TPU v7x, 128 devices: a whole 4x4x4 slice. The times are simulated.
128 devices in a mesh: row: 16 (over x, z_hi, core), col: 8 (over z_lo, y).
Axes of the slice: x: 4, y: 4, z: 4 (z_hi: 2, z_lo: 2; z = z_hi * 2 + z_lo), core: 2. Of those that a mesh axis runs over, the one named last changes fastest.
Arguments:
- ctrl_start: float32 [65536, 512], P(('row', 'col')), may hold values from -6 to 6
- obsv_start: float32 [65536, 512], P(('row', 'col')), may hold values from -6 to 6
- band_tiles: float32 [65536, 384], P(('row', 'col')), may hold values from -0.15625 to 0.15625
- band_offsets: int32 [512, 3], P(('row', 'col')), may hold values from -2 to 2, as said below
Outputs:
- cross_product: float32 [2048, 2048], P('row', 'col')
Inputs may be any that keep to these rules, and one draw needn't show every extreme that they name: `band_offsets`: the 3 offsets of a tile row are distinct.
All inputs are finite; a program needn't handle non-finite values.
Results may differ from a plain program's by a relative error of at most 0.0003.
Values sent between devices are 32-bit elements; how exact they have to be, the bound alone decides.
A program may use at most 128 MiB of HBM per device.

v0:
```python
import math

import jax
import jax.numpy as jnp
from jax import lax
from jax.sharding import Mesh
from jax.sharding import PartitionSpec as P

TILE = 128
HALO = 2
BAND = 3
ROW_COL = ("row_0", "row_1", "row_2", "col")
ROW = ("row_0", "row_1", "row_2")


def extended(array, sides, width):
    for axis, dim in sides:
        size, length = (lax.axis_size(axis), array.shape[dim])
        up = [(i, (i + 1) % size) for i in range(size - 1)]
        down = [(j, i) for i, j in up]
        last = lax.slice_in_dim(array, length - width, length, axis=dim)
        initial = lax.slice_in_dim(array, 0, width, axis=dim)
        before = lax.ppermute(last, axis, up)
        after = lax.ppermute(initial, axis, down)
        array = jnp.concatenate([before, array, after], axis=dim)
    return array


def passed_along(array, axis, by):
    size = lax.axis_size(axis)
    pairs = [(i, i + by) for i in range(size) if 0 <= i + by < size]
    return lax.ppermute(array, axis, pairs)


def in_blocks(array, dim, size):
    before, after = (array.shape[:dim], array.shape[dim + 1 :])
    return jnp.moveaxis(array.reshape(*before, size, -1, *after), dim, 0)


def scatter_pairs(array, chips, core, dim):
    sizes = (lax.axis_size(chips), lax.axis_size(core))
    tiles = in_blocks(array, dim, sizes[0] * sizes[1])
    inside = tiles.shape[1:]
    tiles = tiles.reshape(*sizes, *inside).swapaxes(0, 1).reshape(-1, *inside)
    tiles = lax.psum_scatter(tiles, core, scatter_dimension=0, tiled=True)
    return lax.psum_scatter(tiles, chips, scatter_dimension=0, tiled=True)[0]


def sent_and_summed(array, axis, dim):
    size = lax.axis_size(axis)
    tiles = lax.all_to_all(in_blocks(array, dim, size), axis, 0, 0, tiled=True)
    return jnp.sum(tiles, axis=0)


def forward(field, tiles, offsets):
    margin = HALO * TILE
    padded = extended(field, ((ROW_COL, 0),), margin)
    results = []
    for index in range(field.shape[0] // TILE):
        parts = []
        for slot in range(BAND):
            start = (index + offsets[index, slot]) * TILE + margin
            parts.append(lax.dynamic_slice_in_dim(padded, start, TILE, 0))
        stacked = jnp.concatenate(parts, 0)
        results.append(
            jnp.dot(
                tiles[index * TILE : (index + 1) * TILE],
                stacked,
                precision=lax.Precision.HIGHEST,
                preferred_element_type=jnp.float32,
            )
        )
    return jnp.concatenate(results, 0)


def transpose(field, tiles, offsets):
    total = field.shape[0]
    margin = HALO * TILE
    padded = jnp.zeros((total + 2 * margin, field.shape[1]), jnp.float32)
    for index in range(total // TILE):
        piece = field[index * TILE : (index + 1) * TILE]
        terms = jnp.dot(
            tiles[index * TILE : (index + 1) * TILE].T,
            piece,
            precision=lax.Precision.HIGHEST,
            preferred_element_type=jnp.float32,
        )
        for slot in range(BAND):
            start = (index + offsets[index, slot]) * TILE + margin
            current = lax.dynamic_slice_in_dim(padded, start, TILE, 0)
            padded = lax.dynamic_update_slice_in_dim(
                padded, current + terms[slot * TILE : (slot + 1) * TILE], start, 0
            )
    lower = padded[:margin]
    upper = padded[total + margin :]
    middle = padded[margin : total + margin]
    from_above = passed_along(lower, ROW_COL, -1)
    from_below = passed_along(upper, ROW_COL, 1)
    middle = middle.at[:margin].add(from_below)
    middle = middle.at[total - margin :].add(from_above)
    return middle


def local(ctrl_start, obsv_start, band_tiles, band_offsets):
    ctrl_one = jnp.concatenate([ctrl_start, forward(ctrl_start, band_tiles, band_offsets)], 1)
    ctrl_two = jnp.concatenate(
        [ctrl_one, forward(forward(ctrl_one, band_tiles, band_offsets), band_tiles, band_offsets)],
        1,
    )
    obsv_one = jnp.concatenate([obsv_start, transpose(obsv_start, band_tiles, band_offsets)], 1)
    obsv_two = jnp.concatenate(
        [
            obsv_one,
            transpose(transpose(obsv_one, band_tiles, band_offsets), band_tiles, band_offsets),
        ],
        1,
    )
    rows_here = ctrl_two.shape[0]
    columns = ctrl_two.shape[1]
    row_count = lax.axis_size(ROW)
    col_count = lax.axis_size("col")
    left = obsv_two.reshape(rows_here, row_count, columns // row_count)
    right = ctrl_two.reshape(rows_here, col_count, columns // col_count)
    partial_sum = jnp.einsum(
        "nra,ncb->rcab",
        left,
        right,
        precision=lax.Precision.HIGHEST,
        preferred_element_type=jnp.float32,
    )
    partial_sum = partial_sum.reshape(
        row_count * col_count * (columns // row_count), columns // col_count
    )
    slab = scatter_pairs(partial_sum, ("row_0", "row_1"), "row_2", 0)
    block = sent_and_summed(slab, "col", 0)
    return block * (1.0 / math.sqrt(rows_here * row_count * col_count))


def solution(mesh):
    finer = Mesh(
        mesh.devices.reshape(4, 2, 2, mesh.shape["col"]), ("row_0", "row_1", "row_2", "col")
    )
    placed = (P(ROW_COL, None), P(ROW_COL, None), P(ROW_COL, None), P(ROW_COL, None))
    return jax.shard_map(
        local, mesh=finer, in_specs=placed, out_specs=P(ROW, "col"), check_vma=False
    )
```

profile of v0, /device:TPU:0, one launch (start us, length us, event | category | flops | bytes accessed | tf_op | source)
XLA Modules:
  0.0 434.5 jit_solution(18066372391140527339)
XLA Ops:
  6.5 1.8 fusion.193
  15.8 1.9 fusion.147
  17.7 2.8 fusion.145
  20.5 1.8 fusion.143
  25.1 3.8 collective-permute-start.6
  30.3 4.6 %collective-permute-start = (f32[256,512]{1,0:T(8,128)S(1)}, f32[256,512]{1,0:T(8,128)S(1)}, u32[]{:S(2)}, u32[]{:S(2)}) collective-permute-start(f32[256,512]{1,0:T(8,128)S(1)} %get-tuple-element.122), channel_id=1, source_target_pairs={{0,1},{1,2},{2,3},{3,4},{4,5},{5,6},{6,7},{7,8},{8,9},{9,10},{10,1... | collective-permute-start | bytes 1572872 | tf_op jit(solution)/shard_map/ppermute | solution.py:23
  34.9 1.5 collective-permute-start.1
  36.4 4.7 %collective-permute-done.6 = f32[256,512]{1,0:T(8,128)S(1)} collective-permute-done((f32[256,512]{1,0:T(8,128)S(1)}, f32[256,512]{1,0:T(8,128)S(1)}, u32[]{:S(2)}, u32[]{:S(2)}) %collective-permute-start.6) | collective-permute-done | bytes 524320 | tf_op jit(solution)/shard_map/ppermute | solution.py:32
  41.2 4.3 %collective-permute-done.7 = f32[256,512]{1,0:T(8,128)S(1)} collective-permute-done((f32[256,512]{1,0:T(8,128)S(1)}, f32[256,512]{1,0:T(8,128)S(1)}, u32[]{:S(2)}, u32[]{:S(2)}) %collective-permute-start.7) | collective-permute-done | bytes 524320 | tf_op jit(solution)/shard_map/ppermute | solution.py:32
  45.7 1.4 convolution_bitcast_fusion.8
  47.2 1.4 convolution_bitcast_fusion.7
  48.6 2.6 collective-permute-done
  51.4 1.4 convolution_bitcast_fusion.6
  52.8 1.4 convolution_bitcast_fusion.5
  59.1 1.6 fusion.190
  60.7 4.5 %collective-permute-start.2 = (f32[256,1024]{1,0:T(8,128)}, f32[256,1024]{1,0:T(8,128)}, u32[]{:S(2)}, u32[]{:S(2)}) collective-permute-start(f32[256,1024]{1,0:T(8,128)} %get-tuple-element.105), channel_id=1, source_target_pairs={{0,1},{1,2},{2,3},{3,4},{4,5},{5,6},{6,7},{7,8},{8,9},{9,10},{10,1... | collective-permute-start | bytes 3145736 | tf_op jit(solution)/shard_map/ppermute | solution.py:23
  68.9 2.0 copy-done
  71.9 1.7 collective-permute-start.9
  75.0 1.4 copy.9
  76.4 11.5 %collective-permute-done.2 = f32[256,1024]{1,0:T(8,128)} collective-permute-done((f32[256,1024]{1,0:T(8,128)}, f32[256,1024]{1,0:T(8,128)}, u32[]{:S(2)}, u32[]{:S(2)}) %collective-permute-start.2) | collective-permute-done | bytes 1048608 | tf_op jit(solution)/shard_map/ppermute | solution.py:23
  87.9 5.5 %collective-permute-done.3 = f32[256,1024]{1,0:T(8,128)} collective-permute-done((f32[256,1024]{1,0:T(8,128)}, f32[256,1024]{1,0:T(8,128)}, u32[]{:S(2)}, u32[]{:S(2)}) %collective-permute-start.3) | collective-permute-done | bytes 1048608 | tf_op jit(solution)/shard_map/ppermute | solution.py:24
  93.4 2.3 pad_maximum_fusion
  96.9 17.6 %collective-permute-done.9 = f32[256,1024]{0,1:T(8,128)} collective-permute-done((f32[256,1024]{0,1:T(8,128)}, f32[256,1024]{0,1:T(8,128)}, u32[]{:S(2)}, u32[]{:S(2)}) %collective-permute-start.9) | collective-permute-done | bytes 1048608 | tf_op jit(solution)/shard_map/ppermute | solution.py:32
  114.5 1.5 slice_add_fusion.2
  116.0 3.1 collective-permute-start.8
  121.5 3.6 collective-permute-start.4
  125.1 1.4 convolution_bitcast_fusion.2
  127.9 14.6 %collective-permute-done.8 = f32[256,1024]{0,1:T(8,128)S(1)} collective-permute-done((f32[256,1024]{0,1:T(8,128)S(1)}, f32[256,1024]{0,1:T(8,128)S(1)}, u32[]{:S(2)}, u32[]{:S(2)}) %collective-permute-start.8) | collective-permute-done | bytes 1048608 | tf_op jit(solution)/shard_map/ppermute | solution.py:32
  142.8 1.4 convolution_bitcast_fusion.4
  144.2 1.4 convolution_bitcast_fusion.3
  145.6 19.4 %collective-permute-done.4 = f32[256,1024]{1,0:T(8,128)S(1)} collective-permute-done((f32[256,1024]{1,0:T(8,128)S(1)}, f32[256,1024]{1,0:T(8,128)S(1)}, u32[]{:S(2)}, u32[]{:S(2)}) %collective-permute-start.4) | collective-permute-done | bytes 1048608 | tf_op jit(solution)/shard_map/ppermute | solution.py:23
  171.5 1.5 fusion.189
  173.0 6.0 %collective-permute-start.10 = (f32[256,1024]{0,1:T(8,128)}, f32[256,1024]{0,1:T(8,128)}, u32[]{:S(2)}, u32[]{:S(2)}) collective-permute-start(f32[256,1024]{0,1:T(8,128)} %get-tuple-element.102), channel_id=1, source_target_pairs={{0,1},{1,2},{2,3},{3,4},{4,5},{5,6},{6,7},{7,8},{8,9},{9,10},{10,1... | collective-permute-start | bytes 3145736 | tf_op jit(solution)/shard_map/ppermute | solution.py:32
  179.0 1.5 collective-permute-start.11
  180.6 11.6 %collective-permute-done.5 = f32[256,1024]{1,0:T(8,128)S(1)} collective-permute-done((f32[256,1024]{1,0:T(8,128)S(1)}, f32[256,1024]{1,0:T(8,128)S(1)}, u32[]{:S(2)}, u32[]{:S(2)}) %collective-permute-start.5) | collective-permute-done | bytes 1048608 | tf_op jit(solution)/shard_map/ppermute | solution.py:24
  195.2 2.0 fusion.52
  197.2 2.0 fusion.49
  199.2 4.2 maximum_maximum_fusion
  203.4 2.0 copy.16
  205.3 1.4 fusion.74
  206.8 7.9 %collective-permute-done.11 = f32[256,1024]{0,1:T(8,128)} collective-permute-done((f32[256,1024]{0,1:T(8,128)}, f32[256,1024]{0,1:T(8,128)}, u32[]{:S(2)}, u32[]{:S(2)}) %collective-permute-start.11) | collective-permute-done | bytes 1048608 | tf_op jit(solution)/shard_map/ppermute | solution.py:32
  214.7 1.5 fusion.73
  216.7 29.5 %convolution_bitcast_fusion = f32[16,8,128,256]{3,2,0,1:T(8,128)S(1)} fusion(f32[512,16,128,1]{0,2,1,3:T(8,128)S(1)} %bitcast.83, f32[512,8,256,1]{2,1,0,3:T(8,128)S(1)} %bitcast.82), kind=kOutput, calls=%fused_computation | convolution fusion | flops 25769803776 | bytes 25165824 | tf_op jit(solution)/shard_map/nra,ncb->rcab/dot_general | solution.py:124
  246.2 1.8 copy.11
  248.0 6.1 %copy.12 = f32[2,8,1024,256]{3,2,1,0:T(8,128)} copy(f32[2,8,1024,256]{3,2,0,1:T(8,128)S(1)} %bitcast.80) | data formatting | bytes 33554432 | tf_op jit(solution)/shard_map/transpose | solution.py:44
  254.2 33.2 %reduce-scatter.3.cloned.1.call-done = f32[8,1024,256]{2,1,0:T(8,128)} async-done(((f32[16,1024,256]{2,1,0:T(8,128)}), f32[8,1024,256]{2,1,0:T(8,128)}) %reduce-scatter.3.cloned.1.call-update) | async-done | bytes 8388624 | tf_op jit(solution)/shard_map/reduce_scatter | solution.py:45
  287.4 120.0 %reduce-scatter.5.cloned.1.call-done = f32[1,1024,256]{2,1,0:T(8,128)} async-done(((f32[8,1024,256]{2,1,0:T(8,128)}), f32[1,1024,256]{2,1,0:T(8,128)}) %reduce-scatter.5.cloned.1.call-update) | async-done | bytes 1048592 | tf_op jit(solution)/shard_map/reduce_scatter | solution.py:46
  407.4 19.3 %all_to_all.5 = f32[8,128,256]{2,1,0:T(8,128)S(1)} all-to-all(f32[8,128,256]{2,1,0:T(8,128)} %bitcast.84), channel_id=1, replica_groups=mesh['row_0'=4,'row_1'=2,'row_2'=2,'col'=8] {'col'}, dimensions={0} | all-to-all | bytes 2097152 | tf_op jit(solution)/shard_map/all_to_all | solution.py:51
  (112 shorter events, 31.2 us)
Async XLA Ops:
  6.5 13.9 %copy-start.3 = (f32[512,384]{1,0:T(8,128)S(1)}, f32[512,384]{1,0:T(8,128)}, u32[]{:S(2)}) copy-start(f32[512,384]{1,0:T(8,128)} %param.18) | copy-start | bytes 2359300
  6.5 13.9 %copy-start.2 = (f32[512,512]{1,0:T(8,128)S(1)}, f32[512,512]{1,0:T(8,128)}, u32[]{:S(2)}) copy-start(f32[512,512]{1,0:T(8,128)} %param.17) | copy-start | bytes 3145732
  6.5 280.8 %reduce-scatter.3.cloned.1.call-start = ((), (), s32[]{:S(2)}) async-start(), calls=%async_computation.3 | async-start | bytes 25165824 | tf_op jit(solution)/shard_map/reduce_scatter | solution.py:45
  23.1 1.1 copy-start.13
  23.4 1.2 copy-start.12
  24.8 5.3 %copy-start.4 = (f32[512,512]{1,0:T(8,128)S(1)}, f32[512,512]{1,0:T(8,128)}, u32[]{:S(2)}) copy-start(f32[512,512]{1,0:T(8,128)} %param.16) | copy-start | bytes 3145732
  25.1 16.0 %collective-permute-start.6 = (f32[256,512]{1,0:T(8,128)S(1)}, f32[256,512]{1,0:T(8,128)S(1)}, u32[]{:S(2)}, u32[]{:S(2)}) collective-permute-start(f32[256,512]{1,0:T(8,128)S(1)} %get-tuple-element.120), channel_id=1, source_target_pairs={{0,1},{1,2},{2,3},{3,4},{4,5},{5,6},{6,7},{7,8},{8,9},{9,10},{10,1... | collective-permute-start | bytes 1572872 | tf_op jit(solution)/shard_map/ppermute | solution.py:32
  28.9 16.7 %collective-permute-start.7 = (f32[256,512]{1,0:T(8,128)S(1)}, f32[256,512]{1,0:T(8,128)S(1)}, u32[]{:S(2)}, u32[]{:S(2)}) collective-permute-start(f32[256,512]{1,0:T(8,128)S(1)} %get-tuple-element.119), channel_id=1, source_target_pairs={{1,0},{2,1},{3,2},{4,3},{5,4},{6,5},{7,6},{8,7},{9,8},{10,9},{11,1... | collective-permute-start | bytes 1572872 | tf_op jit(solution)/shard_map/ppermute | solution.py:32
  30.3 21.0 %collective-permute-start = (f32[256,512]{1,0:T(8,128)S(1)}, f32[256,512]{1,0:T(8,128)S(1)}, u32[]{:S(2)}, u32[]{:S(2)}) collective-permute-start(f32[256,512]{1,0:T(8,128)S(1)} %get-tuple-element.122), channel_id=1, source_target_pairs={{0,1},{1,2},{2,3},{3,4},{4,5},{5,6},{6,7},{7,8},{8,9},{9,10},{10,1... | collective-permute-start | bytes 1572872 | tf_op jit(solution)/shard_map/ppermute | solution.py:23
  34.9 20.5 %collective-permute-start.1 = (f32[256,512]{1,0:T(8,128)S(1)}, f32[256,512]{1,0:T(8,128)S(1)}, u32[]{:S(2)}, u32[]{:S(2)}) collective-permute-start(f32[256,512]{1,0:T(8,128)S(1)} %get-tuple-element.121), channel_id=1, source_target_pairs={{1,0},{2,1},{3,2},{4,3},{5,4},{6,5},{7,6},{8,7},{9,8},{10,9},{11,1... | collective-permute-start | bytes 1572872 | tf_op jit(solution)/shard_map/ppermute | solution.py:24
  57.7 0.9 copy-start.6
  58.4 0.7 copy-start.8
  60.7 27.2 %collective-permute-start.2 = (f32[256,1024]{1,0:T(8,128)}, f32[256,1024]{1,0:T(8,128)}, u32[]{:S(2)}, u32[]{:S(2)}) collective-permute-start(f32[256,1024]{1,0:T(8,128)} %get-tuple-element.105), channel_id=1, source_target_pairs={{0,1},{1,2},{2,3},{3,4},{4,5},{5,6},{6,7},{7,8},{8,9},{9,10},{10,1... | collective-permute-start | bytes 3145736 | tf_op jit(solution)/shard_map/ppermute | solution.py:23
  65.1 28.2 %collective-permute-start.3 = (f32[256,1024]{1,0:T(8,128)}, f32[256,1024]{1,0:T(8,128)}, u32[]{:S(2)}, u32[]{:S(2)}) collective-permute-start(f32[256,1024]{1,0:T(8,128)} %get-tuple-element.106), channel_id=1, source_target_pairs={{1,0},{2,1},{3,2},{4,3},{5,4},{6,5},{7,6},{8,7},{9,8},{10,9},{11,1... | collective-permute-start | bytes 3145736 | tf_op jit(solution)/shard_map/ppermute | solution.py:24
  68.8 2.0 copy-start
  71.9 42.5 %collective-permute-start.9 = (f32[256,1024]{0,1:T(8,128)}, f32[256,1024]{0,1:T(8,128)}, u32[]{:S(2)}, u32[]{:S(2)}) collective-permute-start(f32[256,1024]{0,1:T(8,128)} %slice.565), channel_id=1, source_target_pairs={{1,0},{2,1},{3,2},{4,3},{5,4},{6,5},{7,6},{8,7},{9,8},{10,9},{11,1... | collective-permute-start | bytes 3145736 | tf_op jit(solution)/shard_map/ppermute | solution.py:32
  75.0 18.4 %copy-start.5 = (f32[512,512]{1,0:T(8,128)S(1)}, f32[512,512]{1,0:T(8,128)}, u32[]{:S(2)}) copy-start(f32[512,512]{1,0:T(8,128)} %param.16) | copy-start | bytes 3145732
  95.7 18.8 %copy-start.1 = (f32[1024,1024]{0,1:T(8,128)S(1)}, f32[1024,1024]{0,1:T(8,128)}, u32[]{:S(2)}) copy-start(f32[1024,1024]{0,1:T(8,128)} %copy-done) | copy-start | bytes 12582916
  116.0 26.5 %collective-permute-start.8 = (f32[256,1024]{0,1:T(8,128)S(1)}, f32[256,1024]{0,1:T(8,128)S(1)}, u32[]{:S(2)}, u32[]{:S(2)}) collective-permute-start(f32[256,1024]{0,1:T(8,128)S(1)} %get-tuple-element.104), channel_id=1, source_target_pairs={{0,1},{1,2},{2,3},{3,4},{4,5},{5,6},{6,7},{7,8},{8,9},{9,10},{10,1... | collective-permute-start | bytes 3145736 | tf_op jit(solution)/shard_map/ppermute | solution.py:32
  121.5 43.5 %collective-permute-start.4 = (f32[256,1024]{1,0:T(8,128)S(1)}, f32[256,1024]{1,0:T(8,128)S(1)}, u32[]{:S(2)}, u32[]{:S(2)}) collective-permute-start(f32[256,1024]{1,0:T(8,128)S(1)} %pad_maximum_fusion.2), channel_id=1, source_target_pairs={{0,1},{1,2},{2,3},{3,4},{4,5},{5,6},{6,7},{7,8},{8,9},{9,10},{10,1... | collective-permute-start | bytes 3145736 | tf_op jit(solution)/shard_map/ppermute | solution.py:23
  167.5 24.6 %collective-permute-start.5 = (f32[256,1024]{1,0:T(8,128)S(1)}, f32[256,1024]{1,0:T(8,128)S(1)}, u32[]{:S(2)}, u32[]{:S(2)}) collective-permute-start(f32[256,1024]{1,0:T(8,128)S(1)} %pad_maximum_fusion.3), channel_id=1, source_target_pairs={{1,0},{2,1},{3,2},{4,3},{5,4},{6,5},{7,6},{8,7},{9,8},{10,9},{11,1... | collective-permute-start | bytes 3145736 | tf_op jit(solution)/shard_map/ppermute | solution.py:24
  173.0 32.3 %collective-permute-start.10 = (f32[256,1024]{0,1:T(8,128)}, f32[256,1024]{0,1:T(8,128)}, u32[]{:S(2)}, u32[]{:S(2)}) collective-permute-start(f32[256,1024]{0,1:T(8,128)} %get-tuple-element.102), channel_id=1, source_target_pairs={{0,1},{1,2},{2,3},{3,4},{4,5},{5,6},{6,7},{7,8},{8,9},{9,10},{10,1... | collective-permute-start | bytes 3145736 | tf_op jit(solution)/shard_map/ppermute | solution.py:32
  179.0 35.7 %collective-permute-start.11 = (f32[256,1024]{0,1:T(8,128)}, f32[256,1024]{0,1:T(8,128)}, u32[]{:S(2)}, u32[]{:S(2)}) collective-permute-start(f32[256,1024]{0,1:T(8,128)} %get-tuple-element.101), channel_id=1, source_target_pairs={{1,0},{2,1},{3,2},{4,3},{5,4},{6,5},{7,6},{8,7},{9,8},{10,9},{11,1... | collective-permute-start | bytes 3145736 | tf_op jit(solution)/shard_map/ppermute | solution.py:32
  195.2 4.0 copy-start.7
  195.2 3.9 copy-start.9
  206.8 9.4 %copy-start.10 = (f32[512,512]{0,1:T(8,128)S(1)}, f32[512,512]{0,1:T(8,128)}, u32[]{:S(2)}) copy-start(f32[512,512]{0,1:T(8,128)} %copy.8) | copy-start | bytes 3145732
  206.8 9.4 %copy-start.11 = (f32[512,512]{0,1:T(8,128)S(1)}, f32[512,512]{0,1:T(8,128)}, u32[]{:S(2)}) copy-start(f32[512,512]{0,1:T(8,128)} %copy.9) | copy-start | bytes 3145732
  254.1 153.3 %reduce-scatter.5.cloned.1.call-start = ((), (), s32[]{:S(2)}) async-start(), calls=%async_computation.4 | async-start | bytes 9437184 | tf_op jit(solution)/shard_map/reduce_scatter | solution.py:46
Sparse Core Ops, SparseCore 0:
  254.2 33.0 reduce-scatter.2
  291.2 116.1 reduce-scatter.4
where the time goes:
time: 439 us; the launch traced here: 435 us
  waiting for transfers between devices  254 us (58%)
  matrix products  61.6 us (14%)
  starting transfers between devices  34.1 us (8%)
  local copies, waits for them, and re-layouts  26.3 us (6%)
  between operations  22 us (5%)
  blocking collectives  19.3 us (4%)
  other arithmetic  17.1 us (4%)
    reduce_scatter x1, waiting for transfers between devices, scatter_pairs(): return lax.psum_scatter(tiles, chips, scatter_dimension=0, tiled=True)[0]  120 us
    ppermute x6, waiting for transfers between devices, passed_along(): return lax.ppermute(array, axis, pairs)  49.1 us
    ppermute x3, waiting for transfers between devices, extended(): before = lax.ppermute(last, axis, up)  33.6 us
    reduce_scatter x1, waiting for transfers between devices, scatter_pairs(): tiles = lax.psum_scatter(tiles, core, scatter_dimension=0, tiled=True)  33.2 us
    dot_general x1, matrix products, local(): jnp.einsum('nra,ncb->rcab', left, right, precision=lax.Precision.HIGHEST,...  29.5 us
    all_to_all x1, blocking collectives, sent_and_summed(): tiles = lax.all_to_all(in_blocks(array, dim, size), axis, 0, 0, tiled=True)  19.3 us
    dot_general x12, matrix products, transpose(): jnp.dot(tiles[index * TILE:(index + 1) * TILE].T, piece, precision=lax.Pr...  18.5 us
    ppermute x3, waiting for transfers between devices, extended(): after = lax.ppermute(initial, axis, down)  18.2 us
  transfers between devices with their start and end apart: 14, of which 13 were waited for; matrix products, arithmetic and copies ran while one was open for 10% of the time, Pallas kernels for 0%

commit v1 on v0

v1 whole, which is shorter than its diff:
```python
import math

import jax
import jax.numpy as jnp
from jax import lax
from jax.sharding import Mesh
from jax.sharding import PartitionSpec as P

TILE = 128
HALO = 2
BAND = 3
ROW = ("x", "z_hi", "core")
COL = ("z_lo", "y_hi", "y_lo")
ROW_COL = ROW + COL


def extended(array, sides, width):
    for axis, dim in sides:
        size, length = (lax.axis_size(axis), array.shape[dim])
        up = [(i, (i + 1) % size) for i in range(size - 1)]
        down = [(j, i) for i, j in up]
        last = lax.slice_in_dim(array, length - width, length, axis=dim)
        initial = lax.slice_in_dim(array, 0, width, axis=dim)
        before = lax.ppermute(last, axis, up)
        after = lax.ppermute(initial, axis, down)
        array = jnp.concatenate([before, array, after], axis=dim)
    return array


def passed_along(array, axis, by):
    size = lax.axis_size(axis)
    pairs = [(i, i + by) for i in range(size) if 0 <= i + by < size]
    return lax.ppermute(array, axis, pairs)


def forward(field, tiles, offsets):
    margin = HALO * TILE
    padded = extended(field, ((ROW_COL, 0),), margin)
    results = []
    for index in range(field.shape[0] // TILE):
        parts = []
        for slot in range(BAND):
            start = (index + offsets[index, slot]) * TILE + margin
            parts.append(lax.dynamic_slice_in_dim(padded, start, TILE, 0))
        stacked = jnp.concatenate(parts, 0)
        results.append(
            jnp.dot(
                tiles[index * TILE : (index + 1) * TILE],
                stacked,
                precision=lax.Precision.HIGH,
                preferred_element_type=jnp.float32,
            )
        )
    return jnp.concatenate(results, 0)


def transpose(field, tiles, offsets):
    total = field.shape[0]
    margin = HALO * TILE
    padded = jnp.zeros((total + 2 * margin, field.shape[1]), jnp.float32)
    for index in range(total // TILE):
        piece = field[index * TILE : (index + 1) * TILE]
        terms = jnp.dot(
            tiles[index * TILE : (index + 1) * TILE].T,
            piece,
            precision=lax.Precision.HIGH,
            preferred_element_type=jnp.float32,
        )
        for slot in range(BAND):
            start = (index + offsets[index, slot]) * TILE + margin
            current = lax.dynamic_slice_in_dim(padded, start, TILE, 0)
            padded = lax.dynamic_update_slice_in_dim(
                padded, current + terms[slot * TILE : (slot + 1) * TILE], start, 0
            )
    lower = padded[:margin]
    upper = padded[total + margin :]
    middle = padded[margin : total + margin]
    from_above = passed_along(lower, ROW_COL, -1)
    from_below = passed_along(upper, ROW_COL, 1)
    middle = middle.at[:margin].add(from_below)
    middle = middle.at[total - margin :].add(from_above)
    return middle


def hankel(left, right):
    product = jnp.dot(
        left.T, right, precision=lax.Precision.HIGH, preferred_element_type=jnp.float32
    )
    size = product.shape[0] // 4
    half = product.shape[1] // 2
    return product.reshape(4, size, 2, half).transpose(0, 2, 1, 3)


def local(ctrl_start, obsv_start, band_tiles, band_offsets):
    ctrl = [ctrl_start]
    obsv = [obsv_start]
    for step in range(3):
        ctrl.append(forward(ctrl[step], band_tiles, band_offsets))
        obsv.append(transpose(obsv[step], band_tiles, band_offsets))
    blocks = [hankel(obsv[k // 2], ctrl[k - k // 2]) for k in range(7)]
    tiles = jnp.stack(blocks, 0)
    tiles = tiles.reshape(7, 2, 2, 2, *tiles.shape[3:])
    tiles = tiles.transpose(2, 1, 3, 0, 4, 5)
    mine = lax.psum_scatter(tiles, "core", scatter_dimension=0, tiled=True)[0]
    mine = mine.reshape(4, *mine.shape[2:])
    mine = lax.psum_scatter(mine, ("z_hi", "y_lo"), scatter_dimension=0, tiled=True)[0]
    wanted = [x + 2 * z + y for x in range(4) for z in range(2) for y in range(2)]
    spread = jnp.stack([mine[k] for k in wanted], 0)
    block = lax.psum_scatter(spread, ("x", "z_lo", "y_hi"), scatter_dimension=0, tiled=True)[0]
    return block * (1.0 / math.sqrt(ctrl_start.shape[0] * lax.axis_size(ROW_COL)))


def solution(mesh):
    finer = Mesh(mesh.devices.reshape(4, 2, 2, 2, 2, 2), ROW_COL)
    placed = P(ROW_COL, None)
    return jax.shard_map(
        local,
        mesh=finer,
        in_specs=(placed,) * 4,
        out_specs=P(ROW, COL),
        check_vma=False,
    )
```

time: 439 us -> 394 us (0.90)
  local copies, waits for them, and re-layouts: 26.3 us -> 62.5 us
  waiting for transfers between devices: 254 us -> 218 us
  matrix products: 61.6 us -> 31.1 us
  blocking collectives: 19.3 us -> 0 us
  starting transfers between devices: 34.1 us -> 47.8 us
  other arithmetic: 17.1 us -> 11.1 us
    reduce_scatter x2 -> x3, waiting for transfers between devices: 153 us -> 197 us  [the longest x1 92.1 us: local(): lax.psum_scatter(spread, ('x', 'z_lo', 'y_hi'), scatter_dimension=0, tile...]
    ppermute x6, waiting for transfers between devices: 49.1 us -> 11.9 us  [passed_along(): return lax.ppermute(array, axis, pairs)]
    ppermute x3, waiting for transfers between devices: 33.6 us -> 4.12 us  [extended(): before = lax.ppermute(last, axis, up)]
    unnamed x35 -> x113, local copies, waits for them, and re-layouts: 6.96 us -> 27.8 us
    all_to_all x1 -> x0, blocking collectives: 19.3 us -> none  [sent_and_summed(): tiles = lax.all_to_all(in_blocks(array, dim, size), axis, 0, 0, tiled=True)]
    dot_general x1 -> x7, matrix products: 29.5 us -> 11.4 us  [hankel(): jnp.dot(left.T, right, precision=lax.Precision.HIGH, preferred_element_ty...]
    reshape x0 -> x7, local copies, waits for them, and re-layouts: none -> 13.9 us  [hankel(): return product.reshape(4, size, 2, half).transpose(0, 2, 1, 3)]
    ppermute x3, waiting for transfers between devices: 18.2 us -> 4.82 us  [extended(): after = lax.ppermute(initial, axis, down)]
  transfers between devices with their start and end apart: 14 -> 15, of which waited for: 13 -> 8; matrix products, arithmetic and copies ran while one was open for 10% -> 17% of each run, Pallas kernels for 0% -> 0%
where the time goes in v1:
time: 394 us; the launch traced here: 392 us
  waiting for transfers between devices  218 us (55%)
  local copies, waits for them, and re-layouts  62.5 us (16%)
  starting transfers between devices  47.8 us (12%)
  matrix products  31.1 us (8%)
  between operations  21.7 us (6%)
  other arithmetic  11.1 us (3%)
    reduce_scatter x1, waiting for transfers between devices, local(): lax.psum_scatter(spread, ('x', 'z_lo', 'y_hi'), scatter_dimension=0, tile...  92.1 us
    reduce_scatter x1, waiting for transfers between devices, local(): lax.psum_scatter(mine, ('z_hi', 'y_lo'), scatter_dimension=0, tiled=True)[0]  75 us
    reduce_scatter x1, waiting for transfers between devices, local(): mine = lax.psum_scatter(tiles, 'core', scatter_dimension=0, tiled=True)[0]  30.1 us
    unnamed x113, local copies, waits for them, and re-layouts  27.8 us
    ppermute x6, starting transfers between devices, passed_along(): return lax.ppermute(array, axis, pairs)  27 us
    ppermute x3, starting transfers between devices, extended(): before = lax.ppermute(last, axis, up)  16.5 us
    reshape x7, local copies, waits for them, and re-layouts, hankel(): return product.reshape(4, size, 2, half).transpose(0, 2, 1, 3)  13.9 us
    dot_general x12, matrix products, transpose(): jnp.dot(tiles[index * TILE:(index + 1) * TILE].T, piece, precision=lax.Pr...  13.4 us
  transfers between devices with their start and end apart: 15, of which 8 were waited for; matrix products, arithmetic and copies ran while one was open for 17% of the time, Pallas kernels for 0%

profile of v1, /device:TPU:0, one launch (start us, length us, event | category | flops | bytes accessed | tf_op | source)
XLA Modules:
  0.0 392.2 jit_solution(8083017716028995976)
XLA Ops:
  6.5 2.4 fusion.179
  8.9 1.3 collective-permute-start.1
  10.2 5.4 %collective-permute-start = (f32[256,512]{1,0:T(8,128)}, f32[256,512]{1,0:T(8,128)}, u32[]{:S(2)}, u32[]{:S(2)}) collective-permute-start(f32[256,512]{1,0:T(8,128)} %get-tuple-element.124), channel_id=1, source_target_pairs={{0,1},{1,2},{2,3},{3,4},{4,5},{5,6},{6,7},{7,8},{8,9},{9,10},{10,1... | collective-permute-start | bytes 1572872 | tf_op jit(solution)/shard_map/ppermute | solution.py:24
  23.9 1.4 fusion.114
  25.4 1.4 fusion.116
  26.8 1.4 fusion.110
  28.2 1.4 fusion.112
  33.5 1.3 collective-permute-start.3
  34.8 4.6 %collective-permute-start.2 = (f32[256,512]{1,0:T(8,128)}, f32[256,512]{1,0:T(8,128)S(1)}, u32[]{:S(2)}, u32[]{:S(2)}) collective-permute-start(f32[256,512]{1,0:T(8,128)} %get-tuple-element.110), channel_id=1, source_target_pairs={{0,1},{1,2},{2,3},{3,4},{4,5},{5,6},{6,7},{7,8},{8,9},{9,10},{10,1... | collective-permute-start | bytes 1572872 | tf_op jit(solution)/shard_map/ppermute | solution.py:33
  40.5 2.0 fusion.181
  42.5 2.8 reshape.276
  45.3 2.4 copy_dynamic-update-slice_fusion.5
  47.7 1.3 collective-permute-done.2
  56.5 5.1 %collective-permute-start.4 = (f32[256,512]{1,0:T(8,128)S(1)}, f32[256,512]{1,0:T(8,128)S(1)}, u32[]{:S(2)}, u32[]{:S(2)}) collective-permute-start(f32[256,512]{1,0:T(8,128)S(1)} %pad_maximum_fusion.9), channel_id=1, source_target_pairs={{0,1},{1,2},{2,3},{3,4},{4,5},{5,6},{6,7},{7,8},{8,9},{9,10},{10,1... | collective-permute-start | bytes 1572872 | tf_op jit(solution)/shard_map/ppermute | solution.py:24
  64.8 1.3 collective-permute-start.7
  66.1 5.7 %collective-permute-start.6 = (f32[256,512]{1,0:T(8,128)}, f32[256,512]{1,0:T(8,128)}, u32[]{:S(2)}, u32[]{:S(2)}) collective-permute-start(f32[256,512]{1,0:T(8,128)} %get-tuple-element.96), channel_id=1, source_target_pairs={{0,1},{1,2},{2,3},{3,4},{4,5},{5,6},{6,7},{7,8},{8,9},{9,10},{10,1... | collective-permute-start | bytes 1572872 | tf_op jit(solution)/shard_map/ppermute | solution.py:33
  75.8 1.5 collective-permute-start.5
  77.3 2.1 convolution_bitcast_fusion
  79.4 2.5 reshape.277
  81.9 2.3 copy.14
  84.9 1.9 fusion.67
  88.1 1.3 constant_dynamic-update-slice_fusion.16
  89.4 1.4 convolution_bitcast_fusion.2
  92.6 1.7 reshape.278
  94.3 1.4 convolution_bitcast_fusion.1
  95.7 1.4 convolution_bitcast_fusion.3
  97.1 1.9 constant_dynamic-update-slice_fusion.3
  99.0 2.4 constant_dynamic-slice_fusion.15
  102.2 6.0 %collective-permute-start.8 = (f32[256,512]{1,0:T(8,128)S(1)}, f32[256,512]{1,0:T(8,128)S(1)}, u32[]{:S(2)}, u32[]{:S(2)}) collective-permute-start(f32[256,512]{1,0:T(8,128)S(1)} %pad_maximum_fusion.11), channel_id=1, source_target_pairs={{0,1},{1,2},{2,3},{3,4},{4,5},{5,6},{6,7},{7,8},{8,9},{9,10},{10,1... | collective-permute-start | bytes 1572872 | tf_op jit(solution)/shard_map/ppermute | solution.py:24
  108.2 1.4 convolution_bitcast_fusion.4
  110.7 4.1 %collective-permute-done.8 = f32[256,512]{1,0:T(8,128)S(1)} collective-permute-done((f32[256,512]{1,0:T(8,128)S(1)}, f32[256,512]{1,0:T(8,128)S(1)}, u32[]{:S(2)}, u32[]{:S(2)}) %collective-permute-start.8) | collective-permute-done | bytes 524320 | tf_op jit(solution)/shard_map/ppermute | solution.py:24
  117.7 2.0 fusion.62
  119.8 1.3 copy-done.14
  121.1 1.5 collective-permute-start.9
  122.6 1.7 reshape.279
  124.3 1.6 reshape.280
  128.7 4.8 %collective-permute-done.9 = f32[256,512]{1,0:T(8,128)} collective-permute-done((f32[256,512]{1,0:T(8,128)}, f32[256,512]{1,0:T(8,128)}, u32[]{:S(2)}, u32[]{:S(2)}) %collective-permute-start.9) | collective-permute-done | bytes 524320 | tf_op jit(solution)/shard_map/ppermute | solution.py:25
  139.6 12.8 %collective-permute-start.10 = (f32[256,512]{1,0:T(8,128)}, f32[256,512]{1,0:T(8,128)}, u32[]{:S(2)}, u32[]{:S(2)}) collective-permute-start(f32[256,512]{1,0:T(8,128)} %get-tuple-element.82), channel_id=1, source_target_pairs={{0,1},{1,2},{2,3},{3,4},{4,5},{5,6},{6,7},{7,8},{8,9},{9,10},{10,1... | collective-permute-start | bytes 1572872 | tf_op jit(solution)/shard_map/ppermute | solution.py:33
  155.0 2.1 fusion.61
  157.1 2.8 reshape.281
  159.9 1.4 collective-permute-start.11
  161.4 2.3 copy_dynamic-update-slice_fusion.1
  164.8 10.0 %collective-permute-done.11 = f32[256,512]{1,0:T(8,128)S(1)} collective-permute-done((f32[256,512]{1,0:T(8,128)}, f32[256,512]{1,0:T(8,128)S(1)}, u32[]{:S(2)}, u32[]{:S(2)}) %collective-permute-start.11) | collective-permute-done | bytes 524320 | tf_op jit(solution)/shard_map/ppermute | solution.py:33
  178.0 30.1 %reduce-scatter.4.cloned.1.call-done = f32[1,2,2,7,128,256]{5,4,3,2,1,0:T(8,128)} async-done(((f32[2,2,2,7,128,256]{5,4,3,2,1,0:T(8,128)}), f32[1,2,2,7,128,256]{5,4,3,2,1,0:T(8,128)}) %reduce-scatter.4.cloned.1.call-update) | async-done | bytes 3670032 | tf_op jit(solution)/shard_map/reduce_scatter | solution.py:104
  208.1 75.0 %reduce-scatter.6.cloned.1.call-done = f32[1,7,128,256]{3,2,1,0:T(8,128)} async-done(((f32[4,7,128,256]{3,2,1,0:T(8,128)}), f32[1,7,128,256]{3,2,1,0:T(8,128)}) %reduce-scatter.6.cloned.1.call-update) | async-done | bytes 917520 | tf_op jit(solution)/shard_map/reduce_scatter | solution.py:106
  290.7 1.3 copy-done.34
  292.1 92.1 %reduce-scatter.8.cloned.1.call-done = f32[1,128,256]{2,1,0:T(8,128)} async-done(((f32[16,128,256]{2,1,0:T(8,128)}), f32[1,128,256]{2,1,0:T(8,128)}) %reduce-scatter.8.cloned.1.call-update) | async-done | bytes 131088 | tf_op jit(solution)/shard_map/reduce_scatter | solution.py:109
  384.1 1.6 multiply_bitcast_fusion
  (202 shorter events, 51.7 us)
Async XLA Ops:
  6.5 9.1 %copy-start.41 = (s32[4,3]{1,0:T(4,128)S(1)}, s32[4,3]{1,0:T(4,128)}, u32[]{:S(2)}) copy-start(s32[4,3]{1,0:T(4,128)} %param.19) | copy-start | bytes 148
  6.5 17.4 %copy-start = (f32[512,384]{1,0:T(8,128)S(1)}, f32[512,384]{1,0:T(8,128)}, u32[]{:S(2)}) copy-start(f32[512,384]{1,0:T(8,128)} %param.18) | copy-start | bytes 2359300
  6.5 17.4 %copy-start.8 = (f32[512,512]{1,0:T(8,128)S(1)}, f32[512,512]{1,0:T(8,128)}, u32[]{:S(2)}) copy-start(f32[512,512]{1,0:T(8,128)} %param.17) | copy-start | bytes 3145732
  6.5 201.5 %reduce-scatter.4.cloned.1.call-start = ((), (), s32[]{:S(2)}) async-start(), calls=%async_computation.3 | async-start | bytes 11010048 | tf_op jit(solution)/shard_map/reduce_scatter | solution.py:104
  8.9 45.3 %collective-permute-start.1 = (f32[256,512]{1,0:T(8,128)}, f32[256,512]{1,0:T(8,128)}, u32[]{:S(2)}, u32[]{:S(2)}) collective-permute-start(f32[256,512]{1,0:T(8,128)} %get-tuple-element.123), channel_id=1, source_target_pairs={{1,0},{2,1},{3,2},{4,3},{5,4},{6,5},{7,6},{8,7},{9,8},{10,9},{11,1... | collective-permute-start | bytes 1572872 | tf_op jit(solution)/shard_map/ppermute | solution.py:25
  10.2 41.8 %collective-permute-start = (f32[256,512]{1,0:T(8,128)}, f32[256,512]{1,0:T(8,128)}, u32[]{:S(2)}, u32[]{:S(2)}) collective-permute-start(f32[256,512]{1,0:T(8,128)} %get-tuple-element.124), channel_id=1, source_target_pairs={{0,1},{1,2},{2,3},{3,4},{4,5},{5,6},{6,7},{7,8},{8,9},{9,10},{10,1... | collective-permute-start | bytes 1572872 | tf_op jit(solution)/shard_map/ppermute | solution.py:24
  29.6 1.4 copy-start.33
  32.4 8.1 %copy-start.9 = (f32[512,512]{1,0:T(8,128)S(1)}, f32[512,512]{1,0:T(8,128)}, u32[]{:S(2)}) copy-start(f32[512,512]{1,0:T(8,128)} %param.17) | copy-start | bytes 3145732
  32.4 8.0 %copy-start.11 = (f32[512,512]{1,0:T(8,128)S(1)}, f32[512,512]{1,0:T(8,128)}, u32[]{:S(2)}) copy-start(f32[512,512]{1,0:T(8,128)} %param.16) | copy-start | bytes 3145732
  33.5 16.2 %collective-permute-start.3 = (f32[256,512]{1,0:T(8,128)}, f32[256,512]{1,0:T(8,128)}, u32[]{:S(2)}, u32[]{:S(2)}) collective-permute-start(f32[256,512]{1,0:T(8,128)} %get-tuple-element.109), channel_id=1, source_target_pairs={{1,0},{2,1},{3,2},{4,3},{5,4},{6,5},{7,6},{8,7},{9,8},{10,9},{11,1... | collective-permute-start | bytes 1572872 | tf_op jit(solution)/shard_map/ppermute | solution.py:33
  34.8 14.3 %collective-permute-start.2 = (f32[256,512]{1,0:T(8,128)}, f32[256,512]{1,0:T(8,128)S(1)}, u32[]{:S(2)}, u32[]{:S(2)}) collective-permute-start(f32[256,512]{1,0:T(8,128)} %get-tuple-element.110), channel_id=1, source_target_pairs={{0,1},{1,2},{2,3},{3,4},{4,5},{5,6},{6,7},{7,8},{8,9},{9,10},{10,1... | collective-permute-start | bytes 1572872 | tf_op jit(solution)/shard_map/ppermute | solution.py:33
  45.3 3.7 copy-start.4
  50.9 2.8 copy-start.5
  50.9 2.2 copy-start.12
  56.5 15.2 %collective-permute-start.4 = (f32[256,512]{1,0:T(8,128)S(1)}, f32[256,512]{1,0:T(8,128)S(1)}, u32[]{:S(2)}, u32[]{:S(2)}) collective-permute-start(f32[256,512]{1,0:T(8,128)S(1)} %pad_maximum_fusion.9), channel_id=1, source_target_pairs={{0,1},{1,2},{2,3},{3,4},{4,5},{5,6},{6,7},{7,8},{8,9},{9,10},{10,1... | collective-permute-start | bytes 1572872 | tf_op jit(solution)/shard_map/ppermute | solution.py:24
  64.8 23.2 %collective-permute-start.7 = (f32[256,512]{1,0:T(8,128)}, f32[256,512]{1,0:T(8,128)}, u32[]{:S(2)}, u32[]{:S(2)}) collective-permute-start(f32[256,512]{1,0:T(8,128)} %get-tuple-element.95), channel_id=1, source_target_pairs={{1,0},{2,1},{3,2},{4,3},{5,4},{6,5},{7,6},{8,7},{9,8},{10,9},{11,1... | collective-permute-start | bytes 1572872 | tf_op jit(solution)/shard_map/ppermute | solution.py:33
  66.1 18.9 %collective-permute-start.6 = (f32[256,512]{1,0:T(8,128)}, f32[256,512]{1,0:T(8,128)}, u32[]{:S(2)}, u32[]{:S(2)}) collective-permute-start(f32[256,512]{1,0:T(8,128)} %get-tuple-element.96), channel_id=1, source_target_pairs={{0,1},{1,2},{2,3},{3,4},{4,5},{5,6},{6,7},{7,8},{8,9},{9,10},{10,1... | collective-permute-start | bytes 1572872 | tf_op jit(solution)/shard_map/ppermute | solution.py:33
  72.6 4.7 %copy-start.10 = (f32[512,512]{1,0:T(8,128)S(1)}, f32[512,512]{1,0:T(8,128)}, u32[]{:S(2)}) copy-start(f32[512,512]{1,0:T(8,128)} %param.17) | copy-start | bytes 3145732
  73.8 3.5 copy-start.22
  74.9 2.4 copy-start.24
  75.8 21.3 %collective-permute-start.5 = (f32[256,512]{1,0:T(8,128)}, f32[256,512]{1,0:T(8,128)}, u32[]{:S(2)}, u32[]{:S(2)}) collective-permute-start(f32[256,512]{1,0:T(8,128)} %pad_maximum_fusion.10), channel_id=1, source_target_pairs={{1,0},{2,1},{3,2},{4,3},{5,4},{6,5},{7,6},{8,7},{9,8},{10,9},{11,1... | collective-permute-start | bytes 1572872 | tf_op jit(solution)/shard_map/ppermute | solution.py:25
  84.2 2.6 copy-start.6
  84.2 2.6 copy-start.23
  84.2 2.6 copy-start.25
  87.9 2.9 copy-start.19
  89.4 2.5 copy-start.39
  89.4 28.3 %copy-start.2 = (f32[512,512]{1,0:T(8,128)}, f32[512,512]{1,0:T(8,128)S(1)}, u32[]{:S(2)}) copy-start(f32[512,512]{1,0:T(8,128)S(1)} %get-tuple-element.77) | copy-start | bytes 3145732
  92.6 1.7 copy-start.40
  101.3 8.3 %copy-start.18 = (f32[4,128,2,256]{3,2,1,0:T(2,128)S(1)}, f32[4,128,2,256]{3,2,1,0:T(2,128)}, u32[]{:S(2)}) copy-start(f32[4,128,2,256]{3,2,1,0:T(2,128)} %reshape.278) | copy-start | bytes 3145732
  102.2 12.6 %collective-permute-start.8 = (f32[256,512]{1,0:T(8,128)S(1)}, f32[256,512]{1,0:T(8,128)S(1)}, u32[]{:S(2)}, u32[]{:S(2)}) collective-permute-start(f32[256,512]{1,0:T(8,128)S(1)} %pad_maximum_fusion.11), channel_id=1, source_target_pairs={{0,1},{1,2},{2,3},{3,4},{4,5},{5,6},{6,7},{7,8},{8,9},{9,10},{10,1... | collective-permute-start | bytes 1572872 | tf_op jit(solution)/shard_map/ppermute | solution.py:24
  114.9 1.7 copy-start.7
  119.7 4.6 %copy-start.17 = (f32[512,512]{1,0:T(8,128)S(1)}, f32[512,512]{1,0:T(8,128)}, u32[]{:S(2)}) copy-start(f32[512,512]{1,0:T(8,128)} %fusion.62) | copy-start | bytes 3145732
  119.8 1.4 copy-start.14
  121.1 12.4 %collective-permute-start.9 = (f32[256,512]{1,0:T(8,128)}, f32[256,512]{1,0:T(8,128)}, u32[]{:S(2)}, u32[]{:S(2)}) collective-permute-start(f32[256,512]{1,0:T(8,128)} %pad_maximum_fusion.12), channel_id=1, source_target_pairs={{1,0},{2,1},{3,2},{4,3},{5,4},{6,5},{7,6},{8,7},{9,8},{10,9},{11,1... | collective-permute-start | bytes 1572872 | tf_op jit(solution)/shard_map/ppermute | solution.py:25
  124.3 1.6 copy-start.20
  125.9 1.6 copy-start.21
  125.9 7.5 %copy-start.15 = (f32[1024,512]{1,0:T(8,128)S(1)}, f32[1024,512]{1,0:T(8,128)}, u32[]{:S(2)}) copy-start(f32[1024,512]{1,0:T(8,128)} %copy-done.14) | copy-start | bytes 6291460
  128.7 6.2 %copy-start.26 = (f32[384,512]{1,0:T(8,128)S(1)}, f32[384,512]{1,0:T(8,128)}, u32[]{:S(2)}) copy-start(f32[384,512]{1,0:T(8,128)} %convolution_bitcast_fusion.4) | copy-start | bytes 2359300
  139.6 24.1 %collective-permute-start.10 = (f32[256,512]{1,0:T(8,128)}, f32[256,512]{1,0:T(8,128)}, u32[]{:S(2)}, u32[]{:S(2)}) collective-permute-start(f32[256,512]{1,0:T(8,128)} %get-tuple-element.82), channel_id=1, source_target_pairs={{0,1},{1,2},{2,3},{3,4},{4,5},{5,6},{6,7},{7,8},{8,9},{9,10},{10,1... | collective-permute-start | bytes 1572872 | tf_op jit(solution)/shard_map/ppermute | solution.py:33
  152.8 2.2 copy-start.3
  159.9 3.7 copy-start.13
  159.9 14.9 %collective-permute-start.11 = (f32[256,512]{1,0:T(8,128)}, f32[256,512]{1,0:T(8,128)S(1)}, u32[]{:S(2)}, u32[]{:S(2)}) collective-permute-start(f32[256,512]{1,0:T(8,128)} %get-tuple-element.81), channel_id=1, source_target_pairs={{1,0},{2,1},{3,2},{4,3},{5,4},{6,5},{7,6},{8,7},{9,8},{10,9},{11,1... | collective-permute-start | bytes 1572872 | tf_op jit(solution)/shard_map/ppermute | solution.py:33
  163.7 11.4 %copy-start.36 = (f32[128,512]{1,0:T(8,128)S(1)}, f32[128,512]{1,0:T(8,128)}, u32[]{:S(2)}) copy-start(f32[128,512]{1,0:T(8,128)} %copy-done.35) | copy-start | bytes 786436
  163.7 11.4 %copy-start.38 = (f32[128,512]{1,0:T(8,128)S(1)}, f32[128,512]{1,0:T(8,128)}, u32[]{:S(2)}) copy-start(f32[128,512]{1,0:T(8,128)} %copy-done.37) | copy-start | bytes 786436
  177.9 105.2 %reduce-scatter.6.cloned.1.call-start = ((), (), s32[]{:S(2)}) async-start(), calls=%async_computation.4 | async-start | bytes 4587520 | tf_op jit(solution)/shard_map/reduce_scatter | solution.py:106
  208.1 176.1 %reduce-scatter.8.cloned.1.call-start = ((), (), s32[]{:S(2)}) async-start(), calls=%async_computation.5 | async-start | bytes 2228224 | tf_op jit(solution)/shard_map/reduce_scatter | solution.py:109
  283.1 7.4 %copy-start.16 = (f32[1,7,128,256]{3,2,1,0:T(8,128)S(1)}, f32[1,7,128,256]{3,2,1,0:T(8,128)}, u32[]{:S(2)}) copy-start(f32[1,7,128,256]{3,2,1,0:T(8,128)} %reduce-scatter.6.cloned.1.call-done) | copy-start | bytes 2752516
  290.7 1.3 copy-start.34
  (9 other events, 9.7 us)
Sparse Core Ops, SparseCore 0:
  178.0 29.9 reduce-scatter.3
  210.4 72.6 reduce-scatter.5
  292.2 91.9 reduce-scatter.7

commit v2 on v1

v2 whole, which is shorter than its diff:
```python
import math

import jax
import jax.numpy as jnp
from jax import lax
from jax.experimental import pallas as pl
from jax.experimental.pallas import tpu as pltpu
from jax.sharding import PartitionSpec as P

TILE = 128
HALF = 256
ROWS = 512
COLS = 512
ORDER = 65536
BLOCKS = 7
PIECE = 16
MESH = pl.DeviceIdType.MESH
F32 = jnp.float32
BF16 = jnp.bfloat16


def split(value):
    high = value.astype(BF16)
    return high, (value - high.astype(F32)).astype(BF16)


def product(left, right):
    def dot(a, b):
        return jnp.dot(a, b, preferred_element_type=F32)

    return dot(left[0], right[0]) + (dot(left[0], right[1]) + dot(left[1], right[0]))


def kernel(
    ctrl, obsv, band, offsets, out,
    halo_c, halo_o, sent_c, sent_o, part_c, part_o,
    mid_hi, mid_lo, edge_hi, edge_lo, c_hi, c_lo, o_hi, o_lo,
    sent_a, own, got_a, sent_b, got_b, sent_y, got_y, done, got_d,
    hc_send, hc_recv, ho_send, ho_recv, a_send, a_recv, b_send, b_recv, y_send, y_recv, d_sems,
):
    row, col = lax.axis_index("row"), lax.axis_index("col")
    shard = row * 8 + col
    core, z_hi, x = lax.rem(row, 2), lax.rem(lax.div(row, 2), 2), lax.div(row, 4)
    y, z_lo = lax.rem(col, 4), lax.div(col, 4)
    place = x * 4 + z_hi * 2 + z_lo
    before, after = lax.rem(shard + 127, 128), lax.rem(shard + 1, 128)
    before = (lax.div(before, 8), lax.rem(before, 8))
    after = (lax.div(after, 8), lax.rem(after, 8))
    partner = (row + 1 - 2 * core, col)

    def in_plane(d):
        there = lax.rem(place + d, 16)
        xd, zhd, zld = lax.div(there, 4), lax.rem(lax.div(there, 2), 2), lax.rem(there, 2)
        return (xd * 4 + zhd * 2 + core, zld * 4 + y), zhd * TILE + (xd * 2 + zld) * PIECE

    def along_y(d):
        yd = lax.rem(y + d, 4)
        return (row, z_lo * 4 + yd), lax.rem(yd, 2)

    barrier = pltpu.get_barrier_semaphore()
    for device in (before, after, partner):
        pl.semaphore_signal(barrier, inc=1, device_id=device, device_id_type=MESH)

    def greet_plane(d, carry):
        pl.semaphore_signal(barrier, inc=1, device_id=in_plane(d)[0], device_id_type=MESH)
        return carry

    def greet_y(d, carry):
        pl.semaphore_signal(barrier, inc=1, device_id=along_y(d)[0], device_id_type=MESH)
        return carry

    lax.fori_loop(1, 16, greet_plane, 0)
    lax.fori_loop(1, 4, greet_y, 0)
    pl.semaphore_wait(barrier, 21)

    def remote(source, target, send, recv, device):
        return pltpu.make_async_remote_copy(
            src_ref=source,
            dst_ref=target,
            send_sem=send,
            recv_sem=recv,
            device_id=device,
            device_id_type=MESH,
        )

    def exchange(halves, halo, send, recv, k):
        copies = (
            remote(halves[0], halo.at[k, 1], send.at[k, 0], recv.at[k, 1], before),
            remote(halves[1], halo.at[k, 0], send.at[k, 1], recv.at[k, 0], after),
        )
        return copies

    def wait_all(ref, semaphore):
        pltpu.make_async_copy(ref, ref, semaphore).wait()

    c_copies = [
        exchange((src.at[pl.ds(0, HALF)], src.at[pl.ds(HALF, HALF)]), halo_c, hc_send, hc_recv, k)
        for k, src in enumerate((ctrl, sent_c.at[0], sent_c.at[1]))
    ]
    o_copies = [
        exchange((sent_o.at[k, 0], sent_o.at[k, 1]), halo_o, ho_send, ho_recv, k)
        for k in range(3)
    ]
    for copy in c_copies[0]:
        copy.start()

    mid_hi[...] = jnp.zeros_like(mid_hi)
    mid_lo[...] = jnp.zeros_like(mid_lo)
    edge_hi[...] = jnp.zeros_like(edge_hi)
    edge_lo[...] = jnp.zeros_like(edge_lo)
    no_before = 1 - lax.min(shard, 1)
    no_after = lax.div(shard, 127)
    for t in range(4):
        tiles = [band[pl.ds(t * TILE, TILE), pl.ds(b * TILE, TILE)] for b in range(3)]
        for o in range(5):
            e = t + o
            tile = jnp.zeros((TILE, TILE), F32)
            for b in range(3):
                given = offsets[t, b]
                if e < 2:
                    given = given + 100 * no_before
                if e >= 6:
                    given = given + 100 * no_after
                tile = jnp.where(jnp.full((TILE, TILE), given, jnp.int32) == o - 2, tiles[b], tile)
            high, low = split(tile)
            if e < 2:
                to_hi, to_lo, r, c = edge_hi.at[0], edge_lo.at[0], t, e
            elif e < 6:
                to_hi, to_lo, r, c = mid_hi, mid_lo, t, e - 2
            else:
                to_hi, to_lo, r, c = edge_hi.at[1], edge_lo.at[1], t - 2, e - 6
            to_hi[pl.ds(r * TILE, TILE), pl.ds(c * TILE, TILE)] = high
            to_lo[pl.ds(r * TILE, TILE), pl.ds(c * TILE, TILE)] = low

    for q in range(4):
        high, low = split(obsv[:, pl.ds(q * TILE, TILE)].T)
        at = pl.ds((q % 2) * HALF + (q // 2) * TILE, TILE)
        o_hi[at, :] = high
        o_lo[at, :] = low
    c_hi[...], c_lo[...] = split(ctrl[...])

    def send_o(k):
        for h in range(2):
            at = pl.ds(h * HALF, HALF)
            sent_o[k, h] = product((o_hi[:, at], o_lo[:, at]), (edge_hi[h], edge_lo[h]))
            o_copies[k][h].start()

    def mid_o():
        for h in range(2):
            at = pl.ds(h * HALF, HALF)
            part_o[:, at] = product((o_hi[...], o_lo[...]), (mid_hi[:, at], mid_lo[:, at]))

    def mid_c():
        for h in range(2):
            at = pl.ds(h * HALF, HALF)
            part_c[:, at] = product((mid_hi[...], mid_lo[...]), (c_hi[:, at], c_lo[:, at]))

    def next_c(k):
        for h in range(2):
            c_copies[k][1 - h].wait_recv()
            at = pl.ds(h * HALF, HALF)
            value = part_c[at, :] + product((edge_hi[h], edge_lo[h]), split(halo_c[k, h]))
            if k < 2:
                sent_c[k, at, :] = value
                c_copies[k + 1][h].start()
            c_hi[at, :], c_lo[at, :] = split(value)

    def next_o(k):
        for h in range(2):
            o_copies[k][1 - h].wait_recv()
            at = pl.ds(h * HALF, HALF)
            o_hi[:, at], o_lo[:, at] = split(part_o[:, at] + halo_o[k, h])

    def a_copy(k):
        return remote(sent_a.at[k], got_a.at[k], a_send.at[k], a_recv.at[k], partner)

    def block(k):
        def rows_of(which):
            at = pl.ds(pl.multiple_of(which * HALF, HALF), HALF)
            return product((o_hi[at, :], o_lo[at, :]), (c_hi[...], c_lo[...]))

        sent_a[k] = rows_of(1 - core)
        a_copy(k).start()
        own[...] = rows_of(core)

    def plane(k):
        a_copy(k).wait_recv()
        sent_b[k] = own[...] + got_a[k]

        def send(d, carry):
            device, at = in_plane(d)
            remote(
                sent_b.at[k, pl.ds(pl.multiple_of(at, PIECE), PIECE)],
                got_b.at[k, 15 - d],
                b_send.at[k],
                b_recv.at[k],
                device,
            ).start()
            return carry

        lax.fori_loop(1, 16, send, 0)

    def over_y(k):
        wait_all(got_b.at[k], b_recv.at[k])
        at = pl.multiple_of(z_hi * TILE + (x * 2 + z_lo) * PIECE, PIECE)
        total = sent_b[k, pl.ds(at, PIECE), :]
        for i in range(15):
            total = total + got_b[k, i]
        sent_y[k, 0] = total[:, :HALF]
        sent_y[k, 1] = total[:, HALF:]

        def send(d, carry):
            device, half = along_y(d)
            remote(
                sent_y.at[k, half], got_y.at[k, 3 - d], y_send.at[k], y_recv.at[k], device
            ).start()
            return carry

        lax.fori_loop(1, 4, send, 0)

    def finish(k):
        wait_all(got_y.at[k], y_recv.at[k])
        total = sent_y[k, lax.rem(y, 2)] + got_y[k, 0] + got_y[k, 1] + got_y[k, 2]
        done[k] = total * (1.0 / math.sqrt(ORDER))

    send_o(0)
    mid_o()
    block(0)
    mid_c()
    plane(0)

    next_c(0)
    block(1)
    mid_c()
    plane(1)
    over_y(0)

    next_o(0)
    send_o(1)
    block(2)
    mid_o()
    plane(2)
    over_y(1)
    finish(0)

    next_c(1)
    block(3)
    mid_c()
    plane(3)
    over_y(2)
    finish(1)

    next_o(1)
    send_o(2)
    block(4)
    mid_o()
    plane(4)
    over_y(3)
    finish(2)

    next_c(2)
    block(5)
    plane(5)
    over_y(4)
    finish(3)

    next_o(2)
    block(6)
    plane(6)
    over_y(5)
    finish(4)
    over_y(6)
    finish(5)
    finish(6)

    mine = x * 2 + z_lo

    def send_done(d, carry):
        there = lax.rem(mine + d, 8)
        xd, zld = lax.div(there, 2), lax.rem(there, 2)
        remote(
            done.at[xd + 2 * zld + lax.div(y, 2)],
            got_d.at[7 - d],
            d_sems.at[0],
            d_sems.at[1],
            (xd * 4 + z_hi * 2 + core, zld * 4 + y),
        ).start()
        return carry

    lax.fori_loop(1, 8, send_done, 0)
    out[pl.ds(pl.multiple_of(mine * PIECE, PIECE), PIECE), :] = done[
        x + 2 * z_lo + lax.div(y, 2)
    ]
    wait_all(got_d, d_sems.at[1])
    for i in range(7):
        source = lax.rem(mine + 1 + i, 8)
        out[pl.ds(pl.multiple_of(source * PIECE, PIECE), PIECE), :] = got_d[i]

    wait_all(got_d, d_sems.at[0])
    for copies in c_copies + o_copies:
        for copy in copies:
            copy.wait_send()
    for k in range(BLOCKS):
        a_copy(k).wait_send()
        wait_all(got_b.at[k], b_send.at[k])
        wait_all(got_y.at[k], y_send.at[k])


def local(ctrl_start, obsv_start, band_tiles, band_offsets):
    vmem, dma = pltpu.VMEM, pltpu.SemaphoreType.DMA
    return pl.pallas_call(
        kernel,
        out_shape=jax.ShapeDtypeStruct((TILE, HALF), F32),
        in_specs=[pl.BlockSpec(memory_space=pltpu.VMEM)] * 3
        + [pl.BlockSpec(memory_space=pltpu.SMEM)],
        out_specs=pl.BlockSpec(memory_space=pltpu.VMEM),
        scratch_shapes=[
            vmem((3, 2, HALF, COLS), F32),
            vmem((3, 2, COLS, HALF), F32),
            vmem((2, ROWS, COLS), F32),
            vmem((3, 2, COLS, HALF), F32),
            vmem((ROWS, COLS), F32),
            vmem((COLS, ROWS), F32),
            vmem((ROWS, ROWS), BF16),
            vmem((ROWS, ROWS), BF16),
            vmem((2, HALF, HALF), BF16),
            vmem((2, HALF, HALF), BF16),
            vmem((ROWS, COLS), BF16),
            vmem((ROWS, COLS), BF16),
            vmem((COLS, ROWS), BF16),
            vmem((COLS, ROWS), BF16),
            vmem((BLOCKS, HALF, COLS), F32),
            vmem((HALF, COLS), F32),
            vmem((BLOCKS, HALF, COLS), F32),
            vmem((BLOCKS, HALF, COLS), F32),
            vmem((BLOCKS, 15, PIECE, COLS), F32),
            vmem((BLOCKS, 2, PIECE, HALF), F32),
            vmem((BLOCKS, 3, PIECE, HALF), F32),
            vmem((BLOCKS, PIECE, HALF), F32),
            vmem((7, PIECE, HALF), F32),
            dma((3, 2)),
            dma((3, 2)),
            dma((3, 2)),
            dma((3, 2)),
            dma((BLOCKS,)),
            dma((BLOCKS,)),
            dma((BLOCKS,)),
            dma((BLOCKS,)),
            dma((BLOCKS,)),
            dma((BLOCKS,)),
            dma((2,)),
        ],
        compiler_params=pltpu.CompilerParams(
            collective_id=0, has_side_effects=True, vmem_limit_bytes=60 * 1024 * 1024
        ),
    )(ctrl_start, obsv_start, band_tiles, band_offsets)


def solution(mesh):
    placed = P(("row", "col"), None)
    return jax.shard_map(
        local, mesh=mesh, in_specs=(placed,) * 4, out_specs=P("row", "col"), check_vma=False
    )
```

time: 394 us -> 138 us (0.35)
  waiting for transfers between devices: 218 us -> 0 us
  Pallas kernels: 0 us -> 136 us
  local copies, waits for them, and re-layouts: 62.5 us -> 1.57 us
  starting transfers between devices: 47.8 us -> 0 us
  matrix products: 31.1 us -> 0 us
  between operations: 21.7 us -> 0.01 us
  other arithmetic: 11.1 us -> 0 us
    reduce_scatter x3 -> x0, waiting for transfers between devices: 197 us -> none  [the longest x1 92.1 us: local(): lax.psum_scatter(spread, ('x', 'z_lo', 'y_hi'), scatter_dimension=0, tile...]
    pallas_call x0 -> x1, Pallas kernels: none -> 136 us  [local(): pl.pallas_call(kernel, out_shape=jax.ShapeDtypeStruct((TILE, HALF), F32),...]
    ppermute x12 -> x0, starting transfers between devices: 47.8 us -> none  [the longest x6 27 us: passed_along(): return lax.ppermute(array, axis, pairs)]
    dot_general x31 -> x0, matrix products: 31.1 us -> none  [the longest x12 13.4 us: transpose(): jnp.dot(tiles[index * TILE:(index + 1) * TILE].T, piece, precision=lax.Pr...]
    unnamed x113 -> x1, local copies, waits for them, and re-layouts: 27.8 us -> 1.57 us
    ppermute x12 -> x0, waiting for transfers between devices: 20.8 us -> none  [the longest x6 11.9 us: passed_along(): return lax.ppermute(array, axis, pairs)]
    reshape x7 -> x0, local copies, waits for them, and re-layouts: 13.9 us -> none  [hankel(): return product.reshape(4, size, 2, half).transpose(0, 2, 1, 3)]
    slice x8 -> x0, local copies, waits for them, and re-layouts: 9.56 us -> none  [the longest x3 3.27 us: transpose(): middle = padded[margin:total + margin]]
  transfers between devices with their start and end apart: 15 -> 0, of which waited for: 8 -> 0; matrix products, arithmetic and copies ran while one was open for 17% -> 0% of each run, Pallas kernels for 0% -> 0%
where the time goes in v2:
time: 138 us
  Pallas kernels  136 us (99%)
  local copies, waits for them, and re-layouts  1.57 us (1%)
    pallas_call x1, Pallas kernels, local(): pl.pallas_call(kernel, out_shape=jax.ShapeDtypeStruct((TILE, HALF), F32),...  136 us

profile of v2, /device:TPU:0, one launch (start us, length us, event | category | flops | bytes accessed | tf_op | source)
XLA Modules:
  0.0 137.7 jit_solution(14344297753731226457)
XLA Ops:
  0.0 136.1 %shard_map.46 = f32[128,256]{1,0:T(8,128)} custom-call(f32[512,512]{1,0:T(8,128)} %ctrl.1, f32[512,512]{1,0:T(8,128)} %obsv.1, f32[512,384]{1,0:T(8,128)} %band.1, s32[4,3]{1,0:T(4,128)} %offsets.1), custom_call_target="tpu_custom_call" | custom-call | tf_op jit(solution)/shard_map/pallas_call | solution.py:311
  136.1 1.6 %copy.6 = f32[128,256]{1,0:T(8,128)} copy(f32[128,256]{1,0:T(8,128)} %shard_map.46) | data formatting | bytes 262144

commit v3 on v2

--- a/solution.py
+++ b/solution.py
@@ -32,17 +32,20 @@
 
 
 def kernel(
-    ctrl, obsv, band, offsets, out,
+    ctrl_in, obsv_in, band_in, offsets, out, ctrl, obsv, band,
     halo_c, halo_o, sent_c, sent_o, part_c, part_o,
     mid_hi, mid_lo, edge_hi, edge_lo, c_hi, c_lo, o_hi, o_lo,
-    sent_a, own, got_a, sent_b, got_b, sent_y, got_y, done, got_d,
-    hc_send, hc_recv, ho_send, ho_recv, a_send, a_recv, b_send, b_recv, y_send, y_recv, d_sems,
+    sent_a, own, got_a, sent_x, got_x, sent_z, got_z, got_p, sent_y, got_y, done, got_d,
+    in_sems, hc_send, hc_recv, ho_send, ho_recv, last_send, last_recv, a_send, a_recv,
+    x_send, x_recv, z_send, z_recv, p_sems, y_send, y_recv, d_sems,
 ):
     row, col = lax.axis_index("row"), lax.axis_index("col")
     shard = row * 8 + col
     core, z_hi, x = lax.rem(row, 2), lax.rem(lax.div(row, 2), 2), lax.div(row, 4)
     y, z_lo = lax.rem(col, 4), lax.div(col, 4)
     place = x * 4 + z_hi * 2 + z_lo
+    mine = x * 2 + z_lo
+    y_hi = lax.div(y, 2)
     before, after = lax.rem(shard + 127, 128), lax.rem(shard + 1, 128)
     before = (lax.div(before, 8), lax.rem(before, 8))
     after = (lax.div(after, 8), lax.rem(after, 8))
@@ -51,7 +54,7 @@
     def in_plane(d):
         there = lax.rem(place + d, 16)
         xd, zhd, zld = lax.div(there, 4), lax.rem(lax.div(there, 2), 2), lax.rem(there, 2)
-        return (xd * 4 + zhd * 2 + core, zld * 4 + y), zhd * TILE + (xd * 2 + zld) * PIECE
+        return xd * 4 + zhd * 2 + core, zld * 4 + y
 
     def along_y(d):
         yd = lax.rem(y + d, 4)
@@ -62,7 +65,7 @@
         pl.semaphore_signal(barrier, inc=1, device_id=device, device_id_type=MESH)
 
     def greet_plane(d, carry):
-        pl.semaphore_signal(barrier, inc=1, device_id=in_plane(d)[0], device_id_type=MESH)
+        pl.semaphore_signal(barrier, inc=1, device_id=in_plane(d), device_id_type=MESH)
         return carry
 
     def greet_y(d, carry):
@@ -71,6 +74,12 @@
 
     lax.fori_loop(1, 16, greet_plane, 0)
     lax.fori_loop(1, 4, greet_y, 0)
+    inputs = [
+        pltpu.make_async_copy(source, target, in_sems.at[i])
+        for i, (source, target) in enumerate(((band_in, band), (obsv_in, obsv), (ctrl_in, ctrl)))
+    ]
+    for copy in inputs:
+        copy.start()
     pl.semaphore_wait(barrier, 21)
 
     def remote(source, target, send, recv, device):
@@ -95,15 +104,26 @@
 
     c_copies = [
         exchange((src.at[pl.ds(0, HALF)], src.at[pl.ds(HALF, HALF)]), halo_c, hc_send, hc_recv, k)
-        for k, src in enumerate((ctrl, sent_c.at[0], sent_c.at[1]))
+        for k, src in enumerate((ctrl_in, sent_c.at[0], sent_c.at[1]))
     ]
     o_copies = [
         exchange((sent_o.at[k, 0], sent_o.at[k, 1]), halo_o, ho_send, ho_recv, k)
-        for k in range(3)
+        for k in range(2)
     ]
+
+    def last_copy(side, chunk):
+        return remote(
+            sent_o.at[2, side, pl.ds(pl.multiple_of(chunk * TILE, TILE), TILE)],
+            halo_o.at[2, 1 - side, pl.ds(pl.multiple_of(chunk * TILE, TILE), TILE)],
+            last_send.at[side, chunk],
+            last_recv.at[1 - side, chunk],
+            (before, after)[side],
+        )
+
     for copy in c_copies[0]:
         copy.start()
 
+    inputs[0].wait()
     mid_hi[...] = jnp.zeros_like(mid_hi)
     mid_lo[...] = jnp.zeros_like(mid_lo)
     edge_hi[...] = jnp.zeros_like(edge_hi)
@@ -132,11 +152,13 @@
             to_hi[pl.ds(r * TILE, TILE), pl.ds(c * TILE, TILE)] = high
             to_lo[pl.ds(r * TILE, TILE), pl.ds(c * TILE, TILE)] = low
 
+    inputs[1].wait()
     for q in range(4):
         high, low = split(obsv[:, pl.ds(q * TILE, TILE)].T)
         at = pl.ds((q % 2) * HALF + (q // 2) * TILE, TILE)
         o_hi[at, :] = high
         o_lo[at, :] = low
+    inputs[2].wait()
     c_hi[...], c_lo[...] = split(ctrl[...])
 
     def send_o(k):
@@ -144,6 +166,33 @@
             at = pl.ds(h * HALF, HALF)
             sent_o[k, h] = product((o_hi[:, at], o_lo[:, at]), (edge_hi[h], edge_lo[h]))
             o_copies[k][h].start()
+
+    def chunks_for(its_core):
+        return [(1 - its_core) * 2, (1 - its_core) * 2 + 1, its_core * 2, its_core * 2 + 1]
+
+    def rows(chunk):
+        return pl.ds(pl.multiple_of(chunk * TILE, TILE), TILE)
+
+    def send_last_o():
+        orders = [chunks_for(lax.rem(device[0], 2)) for device in (before, after)]
+        for i in range(4):
+            for h in range(2):
+                at = rows(orders[h][i])
+                columns = pl.ds(h * HALF, HALF)
+                sent_o[2, h, at, :] = product(
+                    (o_hi[at, columns], o_lo[at, columns]), (edge_hi[h], edge_lo[h])
+                )
+                last_copy(h, orders[h][i]).start()
+
+    def last_rows(chunk):
+        at = rows(chunk)
+        for h in range(2):
+            last_copy(1 - h, chunk).wait_recv()
+            columns = pl.ds(h * HALF, HALF)
+            o_hi[at, columns], o_lo[at, columns] = split(
+                part_o[at, columns] + halo_o[2, h, at, :]
+            )
+        return product((o_hi[at, :], o_lo[at, :]), (c_hi[...], c_lo[...]))
 
     def mid_o():
         for h in range(2):
@@ -171,8 +220,11 @@
             at = pl.ds(h * HALF, HALF)
             o_hi[:, at], o_lo[:, at] = split(part_o[:, at] + halo_o[k, h])
 
-    def a_copy(k):
-        return remote(sent_a.at[k], got_a.at[k], a_send.at[k], a_recv.at[k], partner)
+    def a_copy(k, z):
+        at = pl.ds(z * TILE, TILE)
+        return remote(
+            sent_a.at[k, at], got_a.at[k, at], a_send.at[k, z], a_recv.at[k, z], partner
+        )
 
     def block(k):
         def rows_of(which):
@@ -180,32 +232,47 @@
             return product((o_hi[at, :], o_lo[at, :]), (c_hi[...], c_lo[...]))
 
         sent_a[k] = rows_of(1 - core)
-        a_copy(k).start()
+        for z in range(2):
+            a_copy(k, z).start()
         own[...] = rows_of(core)
 
-    def plane(k):
-        a_copy(k).wait_recv()
-        sent_b[k] = own[...] + got_a[k]
+    def over_x(k):
+        for z in range(2):
+            a_copy(k, z).wait_recv()
+        sent_x[k] = (own[...] + got_a[k]).reshape(2, 4, 2 * PIECE, COLS)
 
         def send(d, carry):
-            device, at = in_plane(d)
+            xd = lax.rem(x + d, 4)
             remote(
-                sent_b.at[k, pl.ds(pl.multiple_of(at, PIECE), PIECE)],
-                got_b.at[k, 15 - d],
-                b_send.at[k],
-                b_recv.at[k],
-                device,
+                sent_x.at[k, :, xd],
+                got_x.at[k, 3 - d],
+                x_send.at[k],
+                x_recv.at[k],
+                (xd * 4 + z_hi * 2 + core, col),
             ).start()
             return carry
 
-        lax.fori_loop(1, 16, send, 0)
-
-    def over_y(k):
-        wait_all(got_b.at[k], b_recv.at[k])
-        at = pl.multiple_of(z_hi * TILE + (x * 2 + z_lo) * PIECE, PIECE)
-        total = sent_b[k, pl.ds(at, PIECE), :]
-        for i in range(15):
-            total = total + got_b[k, i]
+        lax.fori_loop(1, 4, send, 0)
+
+    def over_z(k):
+        wait_all(got_x.at[k], x_recv.at[k])
+        sent_z[k] = sent_x[k, :, x] + got_x[k, 0] + got_x[k, 1] + got_x[k, 2]
+
+        def send(d, carry):
+            there = lax.rem(z_hi * 2 + z_lo + d, 4)
+            zhd, zld = lax.div(there, 2), lax.rem(there, 2)
+            remote(
+                sent_z.at[k, zhd, pl.ds(pl.multiple_of(zld * PIECE, PIECE), PIECE)],
+                got_z.at[k, 3 - d],
+                z_send.at[k],
+                z_recv.at[k],
+                (x * 4 + zhd * 2 + core, zld * 4 + y),
+            ).start()
+            return carry
+
+        lax.fori_loop(1, 4, send, 0)
+
+    def send_y(k, total):
         sent_y[k, 0] = total[:, :HALF]
         sent_y[k, 1] = total[:, HALF:]
 
@@ -218,79 +285,128 @@
 
         lax.fori_loop(1, 4, send, 0)
 
+    def over_y(k):
+        wait_all(got_z.at[k], z_recv.at[k])
+        at = pl.ds(pl.multiple_of(z_lo * PIECE, PIECE), PIECE)
+        send_y(k, sent_z[k, z_hi, at, :] + got_z[k, 0] + got_z[k, 1] + got_z[k, 2])
+
+    def last_plane(z):
+        same = z_hi if z else 1 - z_hi
+
+        def send(d, carry):
+            there = lax.rem(mine + d, 8)
+            xd, zld = lax.div(there, 2), lax.rem(there, 2)
+
+            @pl.when(d + 1 - same > 0)
+            def _():
+                remote(
+                    sent_x.at[6, z, xd, pl.ds(pl.multiple_of(zld * PIECE, PIECE), PIECE)],
+                    got_p.at[7 + d * (1 - 2 * same)],
+                    p_sems.at[0],
+                    p_sems.at[1],
+                    (xd * 4 + z * 2 + core, zld * 4 + y),
+                ).start()
+
+            return carry
+
+        lax.fori_loop(0, 8, send, 0)
+
+    def last_over_y():
+        wait_all(got_p, p_sems.at[1])
+        total = sent_x[6, z_hi, x, pl.ds(pl.multiple_of(z_lo * PIECE, PIECE), PIECE), :]
+        for i in range(15):
+            total = total + got_p[i]
+        send_y(6, total)
+
     def finish(k):
         wait_all(got_y.at[k], y_recv.at[k])
         total = sent_y[k, lax.rem(y, 2)] + got_y[k, 0] + got_y[k, 1] + got_y[k, 2]
         done[k] = total * (1.0 / math.sqrt(ORDER))
 
+    def send_done(first, last):
+        def send(d, carry):
+            there = lax.rem(mine + d, 8)
+            xd, zld = lax.div(there, 2), lax.rem(there, 2)
+            wanted = xd + 2 * zld + y_hi
+
+            @pl.when(jnp.logical_and(wanted >= first, wanted <= last))
+            def _():
+                remote(
+                    done.at[wanted],
+                    got_d.at[7 - d],
+                    d_sems.at[0],
+                    d_sems.at[1],
+                    (xd * 4 + z_hi * 2 + core, zld * 4 + y),
+                ).start()
+
+            return carry
+
+        lax.fori_loop(1, 8, send, 0)
+
     send_o(0)
     mid_o()
     block(0)
     mid_c()
-    plane(0)
+    over_x(0)
 
     next_c(0)
     block(1)
     mid_c()
-    plane(1)
-    over_y(0)
+    over_x(1)
+    over_z(0)
 
     next_o(0)
     send_o(1)
     block(2)
     mid_o()
-    plane(2)
-    over_y(1)
-    finish(0)
+    over_x(2)
+    over_z(1)
+    over_y(0)
 
     next_c(1)
     block(3)
     mid_c()
-    plane(3)
+    over_x(3)
+    over_z(2)
+    over_y(1)
+    finish(0)
+
+    next_o(1)
+    send_last_o()
+    block(4)
+    mid_o()
+    over_x(4)
+    over_z(3)
     over_y(2)
     finish(1)
 
-    next_o(1)
-    send_o(2)
-    block(4)
-    mid_o()
-    plane(4)
+    next_c(2)
+    block(5)
+    over_x(5)
+    over_z(4)
     over_y(3)
     finish(2)
 
-    next_c(2)
-    block(5)
-    plane(5)
+    for z in range(2):
+        sent_a[6, pl.ds(z * TILE, TILE), :] = last_rows((1 - core) * 2 + z)
+        a_copy(6, z).start()
+    over_z(5)
     over_y(4)
     finish(3)
-
-    next_o(2)
-    block(6)
-    plane(6)
+    for z in range(2):
+        value = last_rows(core * 2 + z)
+        a_copy(6, z).wait_recv()
+        sent_x[6, z] = (value + got_a[6, pl.ds(z * TILE, TILE), :]).reshape(4, 2 * PIECE, COLS)
+        last_plane(z)
     over_y(5)
     finish(4)
-    over_y(6)
     finish(5)
+    send_done(0, 5)
+    last_over_y()
     finish(6)
-
-    mine = x * 2 + z_lo
-
-    def send_done(d, carry):
-        there = lax.rem(mine + d, 8)
-        xd, zld = lax.div(there, 2), lax.rem(there, 2)
-        remote(
-            done.at[xd + 2 * zld + lax.div(y, 2)],
-            got_d.at[7 - d],
-            d_sems.at[0],
-            d_sems.at[1],
-            (xd * 4 + z_hi * 2 + core, zld * 4 + y),
-        ).start()
-        return carry
-
-    lax.fori_loop(1, 8, send_done, 0)
-    out[pl.ds(pl.multiple_of(mine * PIECE, PIECE), PIECE), :] = done[
-        x + 2 * z_lo + lax.div(y, 2)
-    ]
+    send_done(6, 6)
+
+    out[pl.ds(pl.multiple_of(mine * PIECE, PIECE), PIECE), :] = done[x + 2 * z_lo + y_hi]
     wait_all(got_d, d_sems.at[1])
     for i in range(7):
         source = lax.rem(mine + 1 + i, 8)
@@ -300,10 +416,17 @@
     for copies in c_copies + o_copies:
         for copy in copies:
             copy.wait_send()
+    for chunk in range(4):
+        for side in range(2):
+            last_copy(side, chunk).wait_send()
     for k in range(BLOCKS):
-        a_copy(k).wait_send()
-        wait_all(got_b.at[k], b_send.at[k])
+        for z in range(2):
+            a_copy(k, z).wait_send()
         wait_all(got_y.at[k], y_send.at[k])
+        if k < 6:
+            wait_all(got_x.at[k], x_send.at[k])
+            wait_all(got_z.at[k], z_send.at[k])
+    wait_all(got_p, p_sems.at[0])
 
 
 def local(ctrl_start, obsv_start, band_tiles, band_offsets):
@@ -311,10 +434,13 @@
     return pl.pallas_call(
         kernel,
         out_shape=jax.ShapeDtypeStruct((TILE, HALF), F32),
-        in_specs=[pl.BlockSpec(memory_space=pltpu.VMEM)] * 3
+        in_specs=[pl.BlockSpec(memory_space=pl.ANY)] * 3
         + [pl.BlockSpec(memory_space=pltpu.SMEM)],
         out_specs=pl.BlockSpec(memory_space=pltpu.VMEM),
         scratch_shapes=[
+            vmem((ROWS, COLS), F32),
+            vmem((ROWS, COLS), F32),
+            vmem((ROWS, 3 * TILE), F32),
             vmem((3, 2, HALF, COLS), F32),
             vmem((3, 2, COLS, HALF), F32),
             vmem((2, ROWS, COLS), F32),
@@ -332,20 +458,29 @@
             vmem((BLOCKS, HALF, COLS), F32),
             vmem((HALF, COLS), F32),
             vmem((BLOCKS, HALF, COLS), F32),
-            vmem((BLOCKS, HALF, COLS), F32),
-            vmem((BLOCKS, 15, PIECE, COLS), F32),
+            vmem((BLOCKS, 2, 4, 2 * PIECE, COLS), F32),
+            vmem((6, 3, 2, 2 * PIECE, COLS), F32),
+            vmem((6, 2, 2 * PIECE, COLS), F32),
+            vmem((6, 3, PIECE, COLS), F32),
+            vmem((15, PIECE, COLS), F32),
             vmem((BLOCKS, 2, PIECE, HALF), F32),
             vmem((BLOCKS, 3, PIECE, HALF), F32),
             vmem((BLOCKS, PIECE, HALF), F32),
             vmem((7, PIECE, HALF), F32),
+            dma((3,)),
             dma((3, 2)),
             dma((3, 2)),
-            dma((3, 2)),
-            dma((3, 2)),
-            dma((BLOCKS,)),
-            dma((BLOCKS,)),
-            dma((BLOCKS,)),
-            dma((BLOCKS,)),
+            dma((2, 2)),
+            dma((2, 2)),
+            dma((2, 4)),
+            dma((2, 4)),
+            dma((BLOCKS, 2)),
+            dma((BLOCKS, 2)),
+            dma((6,)),
+            dma((6,)),
+            dma((6,)),
+            dma((6,)),
+            dma((2,)),
             dma((BLOCKS,)),
             dma((BLOCKS,)),
             dma((2,)),

time: 138 us -> 111 us (0.80)
  Pallas kernels: 136 us -> 110 us
    pallas_call x1, Pallas kernels: 136 us -> 110 us  [local(): pl.pallas_call(kernel, out_shape=jax.ShapeDtypeStruct((TILE, HALF), F32),...]
where the time goes in v3:
time: 111 us
  Pallas kernels  110 us (99%)
  local copies, waits for them, and re-layouts  1.57 us (1%)
    pallas_call x1, Pallas kernels, local(): pl.pallas_call(kernel, out_shape=jax.ShapeDtypeStruct((TILE, HALF), F32),...  110 us

profile of v3, /device:TPU:0, one launch (start us, length us, event | category | flops | bytes accessed | tf_op | source)
XLA Modules:
  0.0 111.1 jit_solution(10569897297250559948)
XLA Ops:
  0.0 109.6 %shard_map.46 = f32[128,256]{1,0:T(8,128)} custom-call(f32[512,512]{1,0:T(8,128)} %ctrl_in.1, f32[512,512]{1,0:T(8,128)} %obsv_in.1, f32[512,384]{1,0:T(8,128)} %band_in.1, s32[4,3]{1,0:T(4,128)} %offsets.1), custom_call_target="tpu_custom_call" | custom-call | tf_op jit(solution)/shard_map/pallas_call | solution.py:434
  109.6 1.6 %copy.6 = f32[128,256]{1,0:T(8,128)} copy(f32[128,256]{1,0:T(8,128)} %shard_map.46) | data formatting | bytes 262144

commit v4 on v3

--- a/solution.py
+++ b/solution.py
@@ -35,7 +35,7 @@
     ctrl_in, obsv_in, band_in, offsets, out, ctrl, obsv, band,
     halo_c, halo_o, sent_c, sent_o, part_c, part_o,
     mid_hi, mid_lo, edge_hi, edge_lo, c_hi, c_lo, o_hi, o_lo,
-    sent_a, own, got_a, sent_x, got_x, sent_z, got_z, got_p, sent_y, got_y, done, got_d,
+    sent_a, own, got_a, sent_x, got_x, sent_z, ring_z, got_z, got_p, sent_y, got_y, done, got_d,
     in_sems, hc_send, hc_recv, ho_send, ho_recv, last_send, last_recv, a_send, a_recv,
     x_send, x_recv, z_send, z_recv, p_sems, y_send, y_recv, d_sems,
 ):
@@ -254,9 +254,32 @@
 
         lax.fori_loop(1, 4, send, 0)
 
+    z_ring = z_hi * 2 + z_lo
+    z_way = 2 * y_hi - 1
+    z_next = lax.rem(z_ring + z_way + 4, 4)
+    z_after = (x * 4 + lax.div(z_next, 2) * 2 + core, lax.rem(z_next, 2) * 4 + y)
+
+    def z_piece(k, which):
+        at = pl.ds(pl.multiple_of(lax.rem(which, 2) * PIECE, PIECE), PIECE)
+        return sent_z.at[k, lax.div(which, 2), at]
+
+    def ring_copy(k, t):
+        which = lax.rem(z_ring - (t + 1) * z_way + 8, 4)
+        source = ring_z.at[k, t - 1] if t else z_piece(k, which)
+        return remote(source, got_z.at[k, t], z_send.at[k, t], z_recv.at[k, t], z_after)
+
+    def ring(k, t):
+        which = lax.rem(z_ring - (t + 1) * z_way + 8, 4)
+        ring_copy(k, t - 1).wait_recv()
+        ring_z[k, t - 1] = z_piece(k, which)[...] + got_z[k, t - 1]
+        ring_copy(k, t).start()
+
     def over_z(k):
         wait_all(got_x.at[k], x_recv.at[k])
         sent_z[k] = sent_x[k, :, x] + got_x[k, 0] + got_x[k, 1] + got_x[k, 2]
+        if k < 4:
+            ring_copy(k, 0).start()
+            return
 
         def send(d, carry):
             there = lax.rem(z_hi * 2 + z_lo + d, 4)
@@ -264,8 +287,8 @@
             remote(
                 sent_z.at[k, zhd, pl.ds(pl.multiple_of(zld * PIECE, PIECE), PIECE)],
                 got_z.at[k, 3 - d],
-                z_send.at[k],
-                z_recv.at[k],
+                z_send.at[k, 0],
+                z_recv.at[k, 0],
                 (x * 4 + zhd * 2 + core, zld * 4 + y),
             ).start()
             return carry
@@ -286,9 +309,13 @@
         lax.fori_loop(1, 4, send, 0)
 
     def over_y(k):
-        wait_all(got_z.at[k], z_recv.at[k])
-        at = pl.ds(pl.multiple_of(z_lo * PIECE, PIECE), PIECE)
-        send_y(k, sent_z[k, z_hi, at, :] + got_z[k, 0] + got_z[k, 1] + got_z[k, 2])
+        total = z_piece(k, z_ring)[...]
+        if k < 4:
+            ring_copy(k, 2).wait_recv()
+            send_y(k, total + got_z[k, 2])
+        else:
+            wait_all(got_z.at[k], z_recv.at[k, 0])
+            send_y(k, total + got_z[k, 0] + got_z[k, 1] + got_z[k, 2])
 
     def last_plane(z):
         same = z_hi if z else 1 - z_hi
@@ -360,51 +387,53 @@
     block(2)
     mid_o()
     over_x(2)
+    ring(0, 1)
     over_z(1)
-    over_y(0)
 
     next_c(1)
     block(3)
     mid_c()
     over_x(3)
+    ring(0, 2)
+    ring(1, 1)
     over_z(2)
-    over_y(1)
-    finish(0)
 
     next_o(1)
     send_last_o()
     block(4)
     mid_o()
     over_x(4)
+    ring(1, 2)
+    ring(2, 1)
     over_z(3)
-    over_y(2)
-    finish(1)
 
     next_c(2)
     block(5)
     over_x(5)
+    ring(2, 2)
+    ring(3, 1)
     over_z(4)
-    over_y(3)
-    finish(2)
 
     for z in range(2):
         sent_a[6, pl.ds(z * TILE, TILE), :] = last_rows((1 - core) * 2 + z)
         a_copy(6, z).start()
-    over_z(5)
-    over_y(4)
-    finish(3)
+    ring(3, 2)
     for z in range(2):
         value = last_rows(core * 2 + z)
         a_copy(6, z).wait_recv()
         sent_x[6, z] = (value + got_a[6, pl.ds(z * TILE, TILE), :]).reshape(4, 2 * PIECE, COLS)
         last_plane(z)
+    over_z(5)
+    for k in range(5):
+        over_y(k)
+    for k in range(5):
+        finish(k)
+    send_done(0, 4)
+    last_over_y()
     over_y(5)
-    finish(4)
+    finish(6)
     finish(5)
-    send_done(0, 5)
-    last_over_y()
-    finish(6)
-    send_done(6, 6)
+    send_done(5, 6)
 
     out[pl.ds(pl.multiple_of(mine * PIECE, PIECE), PIECE), :] = done[x + 2 * z_lo + y_hi]
     wait_all(got_d, d_sems.at[1])
@@ -425,7 +454,11 @@
         wait_all(got_y.at[k], y_send.at[k])
         if k < 6:
             wait_all(got_x.at[k], x_send.at[k])
-            wait_all(got_z.at[k], z_send.at[k])
+        if k < 4:
+            for t in range(3):
+                ring_copy(k, t).wait_send()
+    for k in range(4, 6):
+        wait_all(got_z.at[k], z_send.at[k, 0])
     wait_all(got_p, p_sems.at[0])
 
 
@@ -461,6 +494,7 @@
             vmem((BLOCKS, 2, 4, 2 * PIECE, COLS), F32),
             vmem((6, 3, 2, 2 * PIECE, COLS), F32),
             vmem((6, 2, 2 * PIECE, COLS), F32),
+            vmem((4, 2, PIECE, COLS), F32),
             vmem((6, 3, PIECE, COLS), F32),
             vmem((15, PIECE, COLS), F32),
             vmem((BLOCKS, 2, PIECE, HALF), F32),
@@ -478,8 +512,8 @@
             dma((BLOCKS, 2)),
             dma((6,)),
             dma((6,)),
-            dma((6,)),
-            dma((6,)),
+            dma((6, 3)),
+            dma((6, 3)),
             dma((2,)),
             dma((BLOCKS,)),
             dma((BLOCKS,)),

time: 111 us -> 102 us (0.919)
  the two profiles are of different devices: /device:TPU:0 before, /device:TPU:38 now
where the time goes in v4:
time: 102 us
  Pallas kernels  100 us (98%)
  local copies, waits for them, and re-layouts  1.57 us (2%)
    pallas_call x1, Pallas kernels, local(): pl.pallas_call(kernel, out_shape=jax.ShapeDtypeStruct((TILE, HALF), F32),...  100 us

profile of v4, /device:TPU:38, one launch (start us, length us, event | category | flops | bytes accessed | tf_op | source)
XLA Modules:
  0.0 101.9 jit_solution(10689232144978515463)
XLA Ops:
  0.0 100.3 %shard_map.46 = f32[128,256]{1,0:T(8,128)} custom-call(f32[512,512]{1,0:T(8,128)} %ctrl_in.1, f32[512,512]{1,0:T(8,128)} %obsv_in.1, f32[512,384]{1,0:T(8,128)} %band_in.1, s32[4,3]{1,0:T(4,128)} %offsets.1), custom_call_target="tpu_custom_call" | custom-call | tf_op jit(solution)/shard_map/pallas_call | solution.py:467
  100.3 1.6 %copy.6 = f32[128,256]{1,0:T(8,128)} copy(f32[128,256]{1,0:T(8,128)} %shard_map.46) | data formatting | bytes 262144

commit v5 on v4

--- a/solution.py
+++ b/solution.py
@@ -426,11 +426,11 @@
     over_z(5)
     for k in range(5):
         over_y(k)
+    last_over_y()
+    over_y(5)
     for k in range(5):
         finish(k)
     send_done(0, 4)
-    last_over_y()
-    over_y(5)
     finish(6)
     finish(5)
     send_done(5, 6)

time: 102 us -> 101 us (level)
  the two profiles are of different devices: /device:TPU:38 before, /device:TPU:0 now
where the time goes in v5:
time: 101 us; the launch traced here: 99.3 us
  Pallas kernels  97.7 us (97%)
  local copies, waits for them, and re-layouts  1.57 us (2%)
    pallas_call x1, Pallas kernels, local(): pl.pallas_call(kernel, out_shape=jax.ShapeDtypeStruct((TILE, HALF), F32),...  97.7 us

profile of v5, /device:TPU:0, one launch (start us, length us, event | category | flops | bytes accessed | tf_op | source)
XLA Modules:
  0.0 99.3 jit_solution(4571885801609929373)
XLA Ops:
  0.0 97.7 %shard_map.46 = f32[128,256]{1,0:T(8,128)} custom-call(f32[512,512]{1,0:T(8,128)} %ctrl_in.1, f32[512,512]{1,0:T(8,128)} %obsv_in.1, f32[512,384]{1,0:T(8,128)} %band_in.1, s32[4,3]{1,0:T(4,128)} %offsets.1), custom_call_target="tpu_custom_call" | custom-call | tf_op jit(solution)/shard_map/pallas_call | solution.py:467
  97.7 1.6 %copy.6 = f32[128,256]{1,0:T(8,128)} copy(f32[128,256]{1,0:T(8,128)} %shard_map.46) | data formatting | bytes 262144

commit v6 on v5

--- a/solution.py
+++ b/solution.py
@@ -418,13 +418,15 @@
         sent_a[6, pl.ds(z * TILE, TILE), :] = last_rows((1 - core) * 2 + z)
         a_copy(6, z).start()
     ring(3, 2)
+    for k in range(3):
+        over_y(k)
     for z in range(2):
         value = last_rows(core * 2 + z)
         a_copy(6, z).wait_recv()
         sent_x[6, z] = (value + got_a[6, pl.ds(z * TILE, TILE), :]).reshape(4, 2 * PIECE, COLS)
         last_plane(z)
     over_z(5)
-    for k in range(5):
+    for k in range(3, 5):
         over_y(k)
     last_over_y()
     over_y(5)

time: 101 us -> 101 us (level)
  no operation moved by 1% of the time
where the time goes in v6:
time: 101 us; the launch traced here: 99.4 us
  Pallas kernels  97.8 us (97%)
  local copies, waits for them, and re-layouts  1.57 us (2%)
    pallas_call x1, Pallas kernels, local(): pl.pallas_call(kernel, out_shape=jax.ShapeDtypeStruct((TILE, HALF), F32),...  97.8 us

profile of v6, /device:TPU:0, one launch (start us, length us, event | category | flops | bytes accessed | tf_op | source)
XLA Modules:
  0.0 99.4 jit_solution(9956743473791054239)
XLA Ops:
  0.0 97.8 %shard_map.46 = f32[128,256]{1,0:T(8,128)} custom-call(f32[512,512]{1,0:T(8,128)} %ctrl_in.1, f32[512,512]{1,0:T(8,128)} %obsv_in.1, f32[512,384]{1,0:T(8,128)} %band_in.1, s32[4,3]{1,0:T(4,128)} %offsets.1), custom_call_target="tpu_custom_call" | custom-call | tf_op jit(solution)/shard_map/pallas_call | solution.py:469
  97.9 1.6 %copy.6 = f32[128,256]{1,0:T(8,128)} copy(f32[128,256]{1,0:T(8,128)} %shard_map.46) | data formatting | bytes 262144
